TPU v7x, 32 devices: a whole 2x2x4 slice. The times are simulated.
32 devices in a mesh: sec: 2 (over y), ty: 4 (over x, core), tx: 4 (over z).
Axes of the slice: x: 2, y: 2, z: 4, core: 2. Of those that a mesh axis runs over, the one named last changes fastest.
Arguments:
- images: float32 [2, 1024, 2048], P('sec', 'ty', 'tx'), may hold values from -12 to 12
Outputs:
- relaxed: float32 [2, 2, 16, 32], P('sec', None, 'ty', 'tx')
- cumulative: float32 [2, 2, 16, 32], P('sec', None, 'ty', 'tx')
All inputs are finite; a program needn't handle non-finite values.
Results may differ from a plain program's by a relative error of at most 0.0003.
Values sent between devices are 32-bit elements; how exact they have to be, the bound alone decides.
No kernel may reach another device: no remote copies, remote signals or barrier semaphores. Data moves between devices by JAX's collectives and lax.ppermute only.
A program may use at most 64 MiB of HBM per device.

v0:
```python
import math

import jax
import jax.numpy as jnp
from jax import lax
from jax.sharding import PartitionSpec as P

PATCH = 128
STRIDE = 64


stiffness = 1.0
rate = 0.25


def shifted(value, axis, by):
    length = lax.axis_size(axis)
    pairs = [(i, i + by) for i in range(length) if 0 <= i + by < length]
    return lax.ppermute(value, axis, pairs)


def padded_2(value, sides, width):
    for axis, dim in sides:
        size, length = (lax.axis_size(axis), value.shape[dim])
        up = [(i, (i + 1) % size) for i in range(size - 1)]
        down = [(j, i) for i, j in up]
        last = lax.slice_in_dim(value, length - width, length, axis=dim)
        first = lax.slice_in_dim(value, 0, width, axis=dim)
        before = lax.ppermute(last, axis, up)
        after = lax.ppermute(first, axis, down)
        value = jnp.concatenate([before, value, after], axis=dim)
    return value


def prefix(value, axis, combine, identity):
    length, position = (lax.axis_size(axis), lax.axis_index(axis))
    everything = lax.all_gather(value, axis)
    start = jnp.broadcast_to(jnp.asarray(identity, value.dtype), value.shape)

    def step(k, before):
        reached = k < position
        new = combine(before, everything[k])
        return jnp.where(reached, new, before)

    return lax.fori_loop(0, length, step, start)


def left_apply(table, values):
    return jnp.einsum("jk,snkl->snjl", table, values, precision=lax.Precision.HIGHEST)


def right_apply(values, table):
    return jnp.einsum("snjk,kl->snjl", values, table, precision=lax.Precision.HIGHEST)


def soft_flow(corr):
    count = corr.shape[0]
    scores = corr / PATCH
    weights = jax.nn.softmax(scores.reshape(count, PATCH * PATCH), axis=-1).reshape(
        count, PATCH, PATCH
    )
    offsets = jnp.arange(PATCH)
    offsets = jnp.where(offsets < PATCH // 2, offsets, offsets - PATCH).astype(jnp.float32)
    flow_y = jnp.sum(weights * offsets[:, None], axis=(1, 2))
    flow_x = jnp.sum(weights * offsets[None, :], axis=(1, 2))
    return jnp.stack([flow_y, flow_x])


def band_flow(bands, cosines, sines):
    nodes = bands.shape[2] // STRIDE - 1
    columns = bands.reshape(2, PATCH, nodes + 1, STRIDE)
    pieces = jnp.concatenate([columns[:, :, :-1], columns[:, :, 1:]], axis=3)
    pieces = jnp.transpose(pieces, (0, 2, 1, 3))
    pieces = pieces - jnp.mean(pieces, axis=(2, 3), keepdims=True)
    left_real = left_apply(cosines, pieces)
    left_imag = -left_apply(sines, pieces)
    freq_real = right_apply(left_real, cosines) + right_apply(left_imag, sines)
    freq_imag = right_apply(left_imag, cosines) - right_apply(left_real, sines)
    prod_real = freq_real[0] * freq_real[1] + freq_imag[0] * freq_imag[1]
    prod_imag = freq_real[0] * freq_imag[1] - freq_imag[0] * freq_real[1]
    prods = jnp.stack([prod_real, prod_imag])
    mixed_real = left_apply(cosines, prods[:1]) - left_apply(sines, prods[1:])
    mixed_imag = left_apply(sines, prods[:1]) + left_apply(cosines, prods[1:])
    corr = (right_apply(mixed_real, cosines) - right_apply(mixed_imag, sines))[0] / (PATCH * PATCH)
    return soft_flow(corr)


def lap_of(padded, center):
    return (
        padded[:, :-2, 1:-1]
        + padded[:, 2:, 1:-1]
        + padded[:, 1:-1, :-2]
        + padded[:, 1:-1, 2:]
        - 4.0 * center
    )


def on_device(images):
    own_tile = images[0]
    half = STRIDE // 2
    next_tile = shifted(own_tile, "sec", -1)
    haloed = padded_2(jnp.stack([own_tile, next_tile]), (("ty", 1), ("tx", 2)), half)
    node_rows = own_tile.shape[0] // STRIDE
    node_cols = own_tile.shape[1] // STRIDE
    grid = jnp.arange(PATCH, dtype=jnp.int32)
    angles = (grid[:, None] * grid[None, :] % PATCH).astype(jnp.float32) * (2.0 * math.pi / PATCH)
    cosines = jnp.cos(angles)
    sines = jnp.sin(angles)
    strips = haloed.reshape(2, node_rows + 1, STRIDE, haloed.shape[2])
    bands = jnp.concatenate([strips[:, :-1], strips[:, 1:]], axis=2)
    bands = jnp.transpose(bands, (1, 0, 2, 3))
    rows = lax.map(lambda band: band_flow(band, cosines, sines), bands)
    flow = jnp.transpose(rows, (1, 0, 2))
    keep = (lax.axis_index("sec") < lax.axis_size("sec") - 1).astype(jnp.float32)
    flow = flow * keep
    padded = padded_2(flow, (("ty", 1), ("tx", 2)), 2)
    inner = padded[:, 1:-1, 1:-1]
    first = inner + rate * (stiffness * lap_of(padded, inner) + inner - inner)
    row_ids = lax.axis_index("ty") * node_rows + jnp.arange(-1, node_rows + 1, dtype=jnp.int32)
    col_ids = lax.axis_index("tx") * node_cols + jnp.arange(-1, node_cols + 1, dtype=jnp.int32)
    row_ok = (row_ids >= 0) & (row_ids < node_rows * lax.axis_size("ty"))
    col_ok = (col_ids >= 0) & (col_ids < node_cols * lax.axis_size("tx"))
    inside = (row_ok[:, None] & col_ok[None, :]).astype(jnp.float32)
    first = first * inside[None]
    center = first[:, 1:-1, 1:-1]
    mesh = center + rate * (stiffness * lap_of(first, center) + flow - center)
    earlier = prefix(mesh, "sec", lambda early, late: early + late, jnp.zeros_like(mesh))
    return (mesh[None], earlier[None])


def solution(mesh):
    in_specs = (P("sec", "ty", "tx"),)
    out_specs = (P("sec", None, "ty", "tx"), P("sec", None, "ty", "tx"))
    return jax.shard_map(
        on_device, mesh=mesh, in_specs=in_specs, out_specs=out_specs, check_vma=False
    )
```

profile of v0, /device:TPU:0, one launch (start us, length us, event | category | flops | bytes accessed | tf_op | source)
XLA Modules:
  0.0 138.1 jit_solution(15300468832693044883)
XLA Ops:
  0.6 1.4 %collective-permute-start = (f32[256,512]{1,0:T(8,128)}, f32[256,512]{1,0:T(8,128)S(1)}, u32[]{:S(2)}, u32[]{:S(2)}) collective-permute-start(f32[256,512]{1,0:T(8,128)} %bitcast.166), channel_id=1, source_target_pairs={{16,0},{17,1},{18,2},{19,3},{20,4},{21,5},{22,6},{23,7},{24,8},{25... | collective-permute-start | bytes 1572872 | tf_op jit(solution)/shard_map/ppermute | solution.py:19
  2.1 15.1 %collective-permute-done = f32[256,512]{1,0:T(8,128)S(1)} collective-permute-done((f32[256,512]{1,0:T(8,128)}, f32[256,512]{1,0:T(8,128)S(1)}, u32[]{:S(2)}, u32[]{:S(2)}) %collective-permute-start) | collective-permute-done | bytes 524320 | tf_op jit(solution)/shard_map/ppermute | solution.py:19
  18.1 1.3 collective-permute-start.1
  19.4 1.3 collective-permute-start.2
  20.7 4.4 %collective-permute-done.2 = f32[2,32,512]{2,1,0:T(8,128)S(1)} collective-permute-done((f32[2,32,512]{2,1,0:T(8,128)S(1)}, f32[2,32,512]{2,1,0:T(8,128)S(1)}, u32[]{:S(2)}, u32[]{:S(2)}) %collective-permute-start.2) | collective-permute-done | bytes 131104 | tf_op jit(solution)/shard_map/ppermute | solution.py:30
  25.3 3.5 %collective-permute-start.3 = (f32[2,320,32]{2,1,0:T(8,128)S(1)}, f32[2,320,32]{2,1,0:T(8,128)S(1)}, u32[]{:S(2)}, u32[]{:S(2)}) collective-permute-start(f32[2,320,32]{2,1,0:T(8,128)S(1)} %get-tuple-element.277), channel_id=1, source_target_pairs={{0,1},{1,2},{2,3},{4,5},{5,6},{6,7},{8,9},{9,10},{10,11},{12,13},{... | collective-permute-start | bytes 245768 | tf_op jit(solution)/shard_map/ppermute | solution.py:29
  28.9 1.3 collective-permute-start.4
  30.2 4.1 %collective-permute-done.3 = f32[2,320,32]{2,1,0:T(8,128)S(1)} collective-permute-done((f32[2,320,32]{2,1,0:T(8,128)S(1)}, f32[2,320,32]{2,1,0:T(8,128)S(1)}, u32[]{:S(2)}, u32[]{:S(2)}) %collective-permute-start.3) | collective-permute-done | bytes 81952 | tf_op jit(solution)/shard_map/ppermute | solution.py:29
  34.3 4.7 %collective-permute-done.4 = f32[2,320,32]{2,1,0:T(8,128)S(1)} collective-permute-done((f32[2,320,32]{2,1,0:T(8,128)S(1)}, f32[2,320,32]{2,1,0:T(8,128)S(1)}, u32[]{:S(2)}, u32[]{:S(2)}) %collective-permute-start.4) | collective-permute-done | bytes 81952 | tf_op jit(solution)/shard_map/ppermute | solution.py:30
  39.9 1.7 %maximum_bitcast_fusion.3 = f32[4,2,128,576]{3,2,0,1:T(8,128)} fusion(f32[2,4,64,576]{3,2,1,0:T(8,128)S(1)} %get-tuple-element.276, f32[2,4,64,576]{3,2,1,0:T(8,128)S(1)} %get-tuple-element.275), kind=kLoop, calls=%fused_computation.114 | loop fusion | flops 589824 | bytes 4718592 | tf_op jit(solution)/shard_map/transpose | solution.py:111
  41.6 2.1 %copy.38 = f32[4,2,128,576]{2,3,1,0:T(8,128)S(1)} copy(f32[4,2,128,576]{3,2,0,1:T(8,128)} %maximum_bitcast_fusion.3) | data formatting | bytes 4718592
  43.7 72.9 %while.29 = (s32[]{:T(128)}, f32[4,2,8]{2,0,1:T(4,128)S(1)}, f32[4,2,128,576]{2,3,1,0:T(8,128)S(1)}, s32[]{:T(128)}, s32[]{:T(128)}) while((s32[]{:T(128)}, f32[4,2,8]{2,0,1:T(4,128)S(1)}, f32[4,2,128,576]{2,3,1,0:T(8,128)S(1)}, s32[]{:T(128)}, s32[]{:T(128)}) %tuple.85), condition=%wide.region_6.7_spmd.clone.clone, body=%wide.region_0.6_spmd.clone.clone.sunk | while | flops 3631481344 | bytes 31065956 | solution.py:112
  44.1 1.2 convolution_bitcast_fusion.2
  45.3 1.9 %fusion.193 = f32[2,8,128,128]{3,2,1,0:T(8,128)S(1)} fusion(f32[2,8,128,128]{2,3,1,0:T(8,128)S(1)} %convolution_bitcast_fusion.2), kind=kOutput, calls=%fused_computation.50.clone.1 | convolution fusion | flops 402882560 | bytes 2097152 | tf_op jit(solution)/shard_map/while/body/eval_jaxpr/snjk,kl->snjl/dot_general | solution.py:53
  47.2 1.2 fusion.191
  48.5 1.9 %convolution_add_fusion.3 = f32[2,8,128,128]{3,2,1,0:T(8,128)S(1)} fusion(f32[2,8,128,128]{3,2,1,0:T(8,128)S(1)} %fusion.193, f32[2,8,128,128]{2,3,1,0:T(8,128)S(1)} %fusion.191), kind=kOutput, calls=%fused_computation.3.clone.1 | convolution fusion | flops 403144704 | bytes 3145728 | tf_op jit(solution)/shard_map/while/body/eval_jaxpr/snjk,kl->snjl/dot_general | solution.py:53
  50.4 1.9 %fusion.192 = f32[2,8,128,128]{3,2,1,0:T(8,128)S(1)} fusion(f32[2,8,128,128]{2,3,1,0:T(8,128)S(1)} %fusion.191), kind=kOutput, calls=%fused_computation.48.clone.1 | convolution fusion | flops 402882560 | bytes 2097152 | tf_op jit(solution)/shard_map/while/body/eval_jaxpr/snjk,kl->snjl/dot_general | solution.py:53
  52.4 1.9 %convolution_subtract_fusion.4 = f32[2,8,128,128]{3,2,1,0:T(8,128)S(1)} fusion(f32[2,8,128,128]{3,2,1,0:T(8,128)S(1)} %fusion.192, f32[2,8,128,128]{2,3,1,0:T(8,128)S(1)} %convolution_bitcast_fusion.2), kind=kOutput, calls=%fused_computation.2.clone.1 | convolution fusion | flops 403144704 | bytes 3145728 | tf_op jit(solution)/shard_map/while/body/eval_jaxpr/snjk,kl->snjl/dot_general | solution.py:53
  60.1 1.2 fusion.199
  62.3 1.2 convolution_bitcast_fusion.2
  63.5 1.9 %fusion.193 = f32[2,8,128,128]{3,2,1,0:T(8,128)S(1)} fusion(f32[2,8,128,128]{2,3,1,0:T(8,128)S(1)} %convolution_bitcast_fusion.2), kind=kOutput, calls=%fused_computation.50.clone.1 | convolution fusion | flops 402882560 | bytes 2097152 | tf_op jit(solution)/shard_map/while/body/eval_jaxpr/snjk,kl->snjl/dot_general | solution.py:53
  65.5 1.2 fusion.191
  66.7 1.9 %convolution_add_fusion.3 = f32[2,8,128,128]{3,2,1,0:T(8,128)S(1)} fusion(f32[2,8,128,128]{3,2,1,0:T(8,128)S(1)} %fusion.193, f32[2,8,128,128]{2,3,1,0:T(8,128)S(1)} %fusion.191), kind=kOutput, calls=%fused_computation.3.clone.1 | convolution fusion | flops 403144704 | bytes 3145728 | tf_op jit(solution)/shard_map/while/body/eval_jaxpr/snjk,kl->snjl/dot_general | solution.py:53
  68.6 1.9 %fusion.192 = f32[2,8,128,128]{3,2,1,0:T(8,128)S(1)} fusion(f32[2,8,128,128]{2,3,1,0:T(8,128)S(1)} %fusion.191), kind=kOutput, calls=%fused_computation.48.clone.1 | convolution fusion | flops 402882560 | bytes 2097152 | tf_op jit(solution)/shard_map/while/body/eval_jaxpr/snjk,kl->snjl/dot_general | solution.py:53
  70.6 1.9 %convolution_subtract_fusion.4 = f32[2,8,128,128]{3,2,1,0:T(8,128)S(1)} fusion(f32[2,8,128,128]{3,2,1,0:T(8,128)S(1)} %fusion.192, f32[2,8,128,128]{2,3,1,0:T(8,128)S(1)} %convolution_bitcast_fusion.2), kind=kOutput, calls=%fused_computation.2.clone.1 | convolution fusion | flops 403144704 | bytes 3145728 | tf_op jit(solution)/shard_map/while/body/eval_jaxpr/snjk,kl->snjl/dot_general | solution.py:53
  78.3 1.2 fusion.199
  80.5 1.2 convolution_bitcast_fusion.2
  81.7 1.9 %fusion.193 = f32[2,8,128,128]{3,2,1,0:T(8,128)S(1)} fusion(f32[2,8,128,128]{2,3,1,0:T(8,128)S(1)} %convolution_bitcast_fusion.2), kind=kOutput, calls=%fused_computation.50.clone.1 | convolution fusion | flops 402882560 | bytes 2097152 | tf_op jit(solution)/shard_map/while/body/eval_jaxpr/snjk,kl->snjl/dot_general | solution.py:53
  83.7 1.2 fusion.191
  84.9 1.9 %convolution_add_fusion.3 = f32[2,8,128,128]{3,2,1,0:T(8,128)S(1)} fusion(f32[2,8,128,128]{3,2,1,0:T(8,128)S(1)} %fusion.193, f32[2,8,128,128]{2,3,1,0:T(8,128)S(1)} %fusion.191), kind=kOutput, calls=%fused_computation.3.clone.1 | convolution fusion | flops 403144704 | bytes 3145728 | tf_op jit(solution)/shard_map/while/body/eval_jaxpr/snjk,kl->snjl/dot_general | solution.py:53
  86.9 1.9 %fusion.192 = f32[2,8,128,128]{3,2,1,0:T(8,128)S(1)} fusion(f32[2,8,128,128]{2,3,1,0:T(8,128)S(1)} %fusion.191), kind=kOutput, calls=%fused_computation.48.clone.1 | convolution fusion | flops 402882560 | bytes 2097152 | tf_op jit(solution)/shard_map/while/body/eval_jaxpr/snjk,kl->snjl/dot_general | solution.py:53
  88.8 1.9 %convolution_subtract_fusion.4 = f32[2,8,128,128]{3,2,1,0:T(8,128)S(1)} fusion(f32[2,8,128,128]{3,2,1,0:T(8,128)S(1)} %fusion.192, f32[2,8,128,128]{2,3,1,0:T(8,128)S(1)} %convolution_bitcast_fusion.2), kind=kOutput, calls=%fused_computation.2.clone.1 | convolution fusion | flops 403144704 | bytes 3145728 | tf_op jit(solution)/shard_map/while/body/eval_jaxpr/snjk,kl->snjl/dot_general | solution.py:53
  96.5 1.2 fusion.199
  98.7 1.2 convolution_bitcast_fusion.2
  100.0 1.9 %fusion.193 = f32[2,8,128,128]{3,2,1,0:T(8,128)S(1)} fusion(f32[2,8,128,128]{2,3,1,0:T(8,128)S(1)} %convolution_bitcast_fusion.2), kind=kOutput, calls=%fused_computation.50.clone.1 | convolution fusion | flops 402882560 | bytes 2097152 | tf_op jit(solution)/shard_map/while/body/eval_jaxpr/snjk,kl->snjl/dot_general | solution.py:53
  101.9 1.2 fusion.191
  103.1 1.9 %convolution_add_fusion.3 = f32[2,8,128,128]{3,2,1,0:T(8,128)S(1)} fusion(f32[2,8,128,128]{3,2,1,0:T(8,128)S(1)} %fusion.193, f32[2,8,128,128]{2,3,1,0:T(8,128)S(1)} %fusion.191), kind=kOutput, calls=%fused_computation.3.clone.1 | convolution fusion | flops 403144704 | bytes 3145728 | tf_op jit(solution)/shard_map/while/body/eval_jaxpr/snjk,kl->snjl/dot_general | solution.py:53
  105.1 1.9 %fusion.192 = f32[2,8,128,128]{3,2,1,0:T(8,128)S(1)} fusion(f32[2,8,128,128]{2,3,1,0:T(8,128)S(1)} %fusion.191), kind=kOutput, calls=%fused_computation.48.clone.1 | convolution fusion | flops 402882560 | bytes 2097152 | tf_op jit(solution)/shard_map/while/body/eval_jaxpr/snjk,kl->snjl/dot_general | solution.py:53
  107.0 1.9 %convolution_subtract_fusion.4 = f32[2,8,128,128]{3,2,1,0:T(8,128)S(1)} fusion(f32[2,8,128,128]{3,2,1,0:T(8,128)S(1)} %fusion.192, f32[2,8,128,128]{2,3,1,0:T(8,128)S(1)} %convolution_bitcast_fusion.2), kind=kOutput, calls=%fused_computation.2.clone.1 | convolution fusion | flops 403144704 | bytes 3145728 | tf_op jit(solution)/shard_map/while/body/eval_jaxpr/snjk,kl->snjl/dot_general | solution.py:53
  113.6 1.1 fusion.196
  114.8 1.2 fusion.199
  116.6 4.0 %collective-permute-start.5 = (f32[2,2,8]{2,1,0:T(2,128)S(1)}, f32[2,2,8]{2,1,0:T(2,128)S(1)}, u32[]{:S(2)}, u32[]{:S(2)}) collective-permute-start(f32[2,2,8]{2,1,0:T(2,128)S(1)} %get-tuple-element.283), channel_id=1, source_target_pairs={{0,4},{4,8},{8,12},{1,5},{5,9},{9,13},{2,6},{6,10},{10,14},{3,7},{... | collective-permute-start | bytes 392 | tf_op jit(solution)/shard_map/ppermute | solution.py:29
  120.6 1.3 collective-permute-start.6
  122.0 1.7 %collective-permute-done.6 = f32[2,2,8]{2,1,0:T(2,128)S(1)} collective-permute-done((f32[2,2,8]{2,1,0:T(2,128)S(1)}, f32[2,2,8]{2,1,0:T(2,128)S(1)}, u32[]{:S(2)}, u32[]{:S(2)}) %collective-permute-start.6) | collective-permute-done | bytes 160 | tf_op jit(solution)/shard_map/ppermute | solution.py:30
  123.8 3.5 %collective-permute-start.7 = (f32[2,8,2]{2,1,0:T(8,128)S(1)}, f32[2,8,2]{2,1,0:T(8,128)S(1)}, u32[]{:S(2)}, u32[]{:S(2)}) collective-permute-start(f32[2,8,2]{2,1,0:T(8,128)S(1)} %get-tuple-element.281), channel_id=1, source_target_pairs={{0,1},{1,2},{2,3},{4,5},{5,6},{6,7},{8,9},{9,10},{10,11},{12,13},{... | collective-permute-start | bytes 392 | tf_op jit(solution)/shard_map/ppermute | solution.py:29
  127.2 1.3 collective-permute-start.8
  128.6 4.2 %collective-permute-done.8 = f32[2,8,2]{2,1,0:T(8,128)S(1)} collective-permute-done((f32[2,8,2]{2,1,0:T(8,128)S(1)}, f32[2,8,2]{2,1,0:T(8,128)S(1)}, u32[]{:S(2)}, u32[]{:S(2)}) %collective-permute-start.8) | collective-permute-done | bytes 160 | tf_op jit(solution)/shard_map/ppermute | solution.py:30
  133.1 4.4 %all-gather = f32[4,4,8]{2,1,0:T(4,128)S(1)} all-gather(f32[2,4,8]{2,1,0:T(4,128)S(1)} %fusion.117), channel_id=2, replica_groups=mesh['sec'=2,'ty'=4,'tx'=4] {'sec'}, dimensions={0}, use_global_device_ids=true | all-gather | bytes 768 | tf_op jit(solution)/shard_map/all_gather | solution.py:37
  (87 shorter events, 28.6 us)
Async XLA Ops:
  0.6 24.5 %copy-start = (f32[1,256,512]{2,1,0:T(8,128)S(1)}, f32[1,256,512]{2,1,0:T(8,128)}, u32[]{:S(2)}) copy-start(f32[1,256,512]{2,1,0:T(8,128)} %param.5) | copy-start | bytes 1572868
  0.6 16.6 %collective-permute-start = (f32[256,512]{1,0:T(8,128)}, f32[256,512]{1,0:T(8,128)S(1)}, u32[]{:S(2)}, u32[]{:S(2)}) collective-permute-start(f32[256,512]{1,0:T(8,128)} %bitcast.166), channel_id=1, source_target_pairs={{16,0},{17,1},{18,2},{19,3},{20,4},{21,5},{22,6},{23,7},{24,8},{25... | collective-permute-start | bytes 1572872 | tf_op jit(solution)/shard_map/ppermute | solution.py:19
  18.1 2.6 %collective-permute-start.1 = (f32[2,32,512]{2,1,0:T(8,128)S(1)}, f32[2,32,512]{2,1,0:T(8,128)S(1)}, u32[]{:S(2)}, u32[]{:S(2)}) collective-permute-start(f32[2,32,512]{2,1,0:T(8,128)S(1)} %get-tuple-element.279), channel_id=1, source_target_pairs={{0,4},{4,8},{8,12},{1,5},{5,9},{9,13},{2,6},{6,10},{10,14},{3,7},{... | collective-permute-start | bytes 393224 | tf_op jit(solution)/shard_map/ppermute | solution.py:29
  19.4 5.8 %collective-permute-start.2 = (f32[2,32,512]{2,1,0:T(8,128)S(1)}, f32[2,32,512]{2,1,0:T(8,128)S(1)}, u32[]{:S(2)}, u32[]{:S(2)}) collective-permute-start(f32[2,32,512]{2,1,0:T(8,128)S(1)} %get-tuple-element.280), channel_id=1, source_target_pairs={{4,0},{8,4},{12,8},{5,1},{9,5},{13,9},{6,2},{10,6},{14,10},{7,3},{... | collective-permute-start | bytes 393224 | tf_op jit(solution)/shard_map/ppermute | solution.py:30
  25.3 9.0 %collective-permute-start.3 = (f32[2,320,32]{2,1,0:T(8,128)S(1)}, f32[2,320,32]{2,1,0:T(8,128)S(1)}, u32[]{:S(2)}, u32[]{:S(2)}) collective-permute-start(f32[2,320,32]{2,1,0:T(8,128)S(1)} %get-tuple-element.277), channel_id=1, source_target_pairs={{0,1},{1,2},{2,3},{4,5},{5,6},{6,7},{8,9},{9,10},{10,11},{12,13},{... | collective-permute-start | bytes 245768 | tf_op jit(solution)/shard_map/ppermute | solution.py:29
  28.9 10.2 %collective-permute-start.4 = (f32[2,320,32]{2,1,0:T(8,128)S(1)}, f32[2,320,32]{2,1,0:T(8,128)S(1)}, u32[]{:S(2)}, u32[]{:S(2)}) collective-permute-start(f32[2,320,32]{2,1,0:T(8,128)S(1)} %get-tuple-element.278), channel_id=1, source_target_pairs={{1,0},{2,1},{3,2},{5,4},{6,5},{7,6},{9,8},{10,9},{11,10},{13,12},{... | collective-permute-start | bytes 245768 | tf_op jit(solution)/shard_map/ppermute | solution.py:30
  116.6 5.3 %collective-permute-start.5 = (f32[2,2,8]{2,1,0:T(2,128)S(1)}, f32[2,2,8]{2,1,0:T(2,128)S(1)}, u32[]{:S(2)}, u32[]{:S(2)}) collective-permute-start(f32[2,2,8]{2,1,0:T(2,128)S(1)} %get-tuple-element.283), channel_id=1, source_target_pairs={{0,4},{4,8},{8,12},{1,5},{5,9},{9,13},{2,6},{6,10},{10,14},{3,7},{... | collective-permute-start | bytes 392 | tf_op jit(solution)/shard_map/ppermute | solution.py:29
  120.6 3.1 %collective-permute-start.6 = (f32[2,2,8]{2,1,0:T(2,128)S(1)}, f32[2,2,8]{2,1,0:T(2,128)S(1)}, u32[]{:S(2)}, u32[]{:S(2)}) collective-permute-start(f32[2,2,8]{2,1,0:T(2,128)S(1)} %get-tuple-element.284), channel_id=1, source_target_pairs={{4,0},{8,4},{12,8},{5,1},{9,5},{13,9},{6,2},{10,6},{14,10},{7,3},{... | collective-permute-start | bytes 392 | tf_op jit(solution)/shard_map/ppermute | solution.py:30
  123.8 4.8 %collective-permute-start.7 = (f32[2,8,2]{2,1,0:T(8,128)S(1)}, f32[2,8,2]{2,1,0:T(8,128)S(1)}, u32[]{:S(2)}, u32[]{:S(2)}) collective-permute-start(f32[2,8,2]{2,1,0:T(8,128)S(1)} %get-tuple-element.281), channel_id=1, source_target_pairs={{0,1},{1,2},{2,3},{4,5},{5,6},{6,7},{8,9},{9,10},{10,11},{12,13},{... | collective-permute-start | bytes 392 | tf_op jit(solution)/shard_map/ppermute | solution.py:29
  127.2 5.5 %collective-permute-start.8 = (f32[2,8,2]{2,1,0:T(8,128)S(1)}, f32[2,8,2]{2,1,0:T(8,128)S(1)}, u32[]{:S(2)}, u32[]{:S(2)}) collective-permute-start(f32[2,8,2]{2,1,0:T(8,128)S(1)} %get-tuple-element.282), channel_id=1, source_target_pairs={{1,0},{2,1},{3,2},{5,4},{6,5},{7,6},{9,8},{10,9},{11,10},{13,12},{... | collective-permute-start | bytes 392 | tf_op jit(solution)/shard_map/ppermute | solution.py:30
  133.0 4.4 %copy-start.2 = (f32[2,4,8]{2,1,0:T(4,128)}, f32[2,4,8]{2,1,0:T(4,128)S(1)}, u32[]{:S(2)}) copy-start(f32[2,4,8]{2,1,0:T(4,128)S(1)} %fusion.117) | copy-start | bytes 772
  137.5 0.6 copy-start.1
where the time goes:
time: 138 us
  matrix products  68.1 us (49%)
  waiting for transfers between devices  34.4 us (25%)
  starting transfers between devices  18.8 us (14%)
  other arithmetic  7.25 us (5%)
  blocking collectives  4.36 us (3%)
  local copies, waits for them, and re-layouts  3.84 us (3%)
    dot_general x24, matrix products, right_apply(): jnp.einsum('snjk,kl->snjl', values, table, precision=lax.Precision.HIGHEST)  40.4 us
    dot_general x24, matrix products, left_apply(): jnp.einsum('jk,snkl->snjl', table, values, precision=lax.Precision.HIGHEST)  27.7 us
    ppermute x1, waiting for transfers between devices, shifted(): return lax.ppermute(value, axis, pairs)  15.1 us
    ppermute x4, waiting for transfers between devices, padded_2(): after = lax.ppermute(first, axis, down)  15.1 us
    ppermute x4, starting transfers between devices, padded_2(): before = lax.ppermute(last, axis, up)  12.2 us
    ppermute x4, starting transfers between devices, padded_2(): after = lax.ppermute(first, axis, down)  5.17 us
    all_gather x1, blocking collectives, prefix(): everything = lax.all_gather(value, axis)  4.36 us
    ppermute x4, waiting for transfers between devices, padded_2(): before = lax.ppermute(last, axis, up)  4.17 us
  transfers between devices with their start and end apart: 9, of which 6 were waited for; matrix products, arithmetic and copies ran while one was open for 0% of the time, Pallas kernels for 0%

commit v1 on v0

v1 whole, which is shorter than its diff:
```python
import functools

import jax
import jax.numpy as jnp
import numpy as np
from jax import lax
from jax.experimental import pallas as pl
from jax.experimental.pallas import tpu as pltpu
from jax.sharding import PartitionSpec as P

PATCH = 128
STRIDE = 64
HALF = STRIDE // 2
FREQ = -(-(PATCH // 2 + 1) // 8) * 8

stiffness = 1.0
rate = 0.25


def two_parts(table):
    high = table.astype(jnp.bfloat16)
    low = (table - high.astype(np.float64)).astype(jnp.bfloat16)
    return high, low


def tables():
    angle = 2.0 * np.pi * (np.outer(np.arange(PATCH), np.arange(PATCH)) % PATCH) / PATCH
    cosine, sine = np.cos(angle), np.sin(angle)
    kept = np.arange(FREQ)[:, None] <= PATCH // 2
    left = np.concatenate([cosine[:FREQ] * kept, -sine[:FREQ] * kept])
    right = np.block([[cosine, -sine], [sine, cosine]])
    share = np.where((np.arange(FREQ) == 0) | (np.arange(FREQ) == PATCH // 2), 1.0, 2.0)
    scaled = (share * kept[:, 0])[None, :] / float(PATCH) ** 3
    back = np.concatenate([cosine[:, :FREQ] * scaled, sine[:, :FREQ] * scaled], axis=1)
    left_hi, left_lo = two_parts(left)
    back_hi, back_lo = two_parts(back)
    right_hi, right_lo = two_parts(right)
    return (
        np.concatenate([left_hi, left_hi, left_lo], axis=1),
        np.stack([right_hi, right_lo]),
        np.concatenate([back_hi, back_hi, back_lo], axis=1),
    )


def split(values):
    high = values.astype(jnp.bfloat16)
    return high, (values - high.astype(jnp.float32)).astype(jnp.bfloat16)


def mul(a, b):
    return jnp.dot(a, b, preferred_element_type=jnp.float32)


def right_dft(values, right_ref):
    high, low = split(values)
    return mul(high, right_ref[0]) + mul(low, right_ref[0]) + mul(high, right_ref[1])


def flow_kernel(rows, cols, group, region_ref, left_ref, right_ref, back_ref, flow_ref,
                high_ref, low_ref, half_ref, peak_ref, mass_ref, tilt_ref):
    wide = cols * STRIDE
    for z in range(2):
        even, odd = region_ref[z, :, :wide], region_ref[z, :, STRIDE:STRIDE + wide]
        for part, values in enumerate((even, odd)):
            high, low = split(values)
            high_ref[z, :, part * wide:(part + 1) * wide] = high
            low_ref[z, :, part * wide:(part + 1) * wide] = low
    order = [2 * t for t in range(cols // 2)] + [2 * t + 1 for t in range(cols // 2)]
    for z in range(2):
        for i in range(rows):
            band = pl.ds(i * STRIDE, PATCH)
            high = high_ref[z, band, :]
            stacked = jnp.concatenate([high, low_ref[z, band, :], high], axis=0)
            out = mul(left_ref[...], stacked)
            for t, j in enumerate(order):
                lanes = slice(t * PATCH, (t + 1) * PATCH)
                half_ref[z, i * cols + j, :, :PATCH] = out[:FREQ, lanes]
                half_ref[z, i * cols + j, :, PATCH:] = out[FREQ:, lanes]
    row = lax.broadcasted_iota(jnp.int32, (group, FREQ, PATCH), 1)
    lane = lax.broadcasted_iota(jnp.int32, (group, FREQ, PATCH), 2)
    varies = ((row + lane) > 0).astype(jnp.float32).reshape(group * FREQ, PATCH)
    lag = lax.broadcasted_iota(jnp.int32, (PATCH, 1), 0)
    lag = jnp.where(lag < PATCH // 2, lag, lag - PATCH).astype(jnp.float32)
    for n in range(0, rows * cols, group):
        both = half_ref[:, n:n + group].reshape(2 * group * FREQ, 2 * PATCH)
        freq = right_dft(both, right_ref)
        first, second = freq[:group * FREQ], freq[group * FREQ:]
        re1, im1 = first[:, :PATCH] * varies, first[:, PATCH:] * varies
        re2, im2 = second[:, :PATCH] * varies, second[:, PATCH:] * varies
        cross = jnp.concatenate([re1 * re2 + im1 * im2, im1 * re2 - re1 * im2], axis=1)
        mixed = right_dft(cross, right_ref)
        columns = []
        for m in range(group):
            part = mixed[m * FREQ:(m + 1) * FREQ]
            columns.append(jnp.concatenate([part[:, :PATCH], part[:, PATCH:]], axis=0))
        high, low = split(jnp.concatenate(columns, axis=1))
        scores = mul(back_ref[...], jnp.concatenate([high, low, high], axis=0))
        peak = jnp.max(scores, axis=0, keepdims=True)
        weight = jnp.exp(scores - peak)
        mass = jnp.sum(weight, axis=0, keepdims=True)
        tilt = jnp.sum(weight * lag, axis=0, keepdims=True)
        for m in range(group):
            lanes = slice(m * PATCH, (m + 1) * PATCH)
            peak_ref[n + m:n + m + 1, :] = peak[:, lanes]
            mass_ref[n + m:n + m + 1, :] = mass[:, lanes]
            tilt_ref[n + m:n + m + 1, :] = tilt[:, lanes]
    peak = peak_ref[...]
    share = jnp.exp(peak - jnp.max(peak, axis=1, keepdims=True))
    mass = mass_ref[...] * share
    lag = lax.broadcasted_iota(jnp.int32, mass.shape, 1)
    place = lax.broadcasted_iota(jnp.int32, mass.shape, 0) % cols
    here = lag == place
    lag = jnp.where(lag < PATCH // 2, lag, lag - PATCH).astype(jnp.float32)
    total = jnp.sum(mass, axis=1, keepdims=True)
    flow_y = jnp.sum(tilt_ref[...] * share, axis=1, keepdims=True) / total
    flow_x = jnp.sum(mass * lag, axis=1, keepdims=True) / total
    for c, value in enumerate((flow_y, flow_x)):
        spread = jnp.where(here, value, 0.0)
        for i in range(rows):
            flow_ref[c * rows + i:c * rows + i + 1, :] = jnp.sum(
                spread[i * cols:(i + 1) * cols], axis=0, keepdims=True
            )


def flow_of(region, rows, cols, group=4):
    left, right, back = tables()
    count = rows * cols
    return pl.pallas_call(
        functools.partial(flow_kernel, rows, cols, group),
        out_shape=jax.ShapeDtypeStruct((2 * rows, PATCH), jnp.float32),
        in_specs=[pl.BlockSpec(memory_space=pltpu.VMEM)] * 4,
        out_specs=pl.BlockSpec(memory_space=pltpu.VMEM),
        scratch_shapes=[
            pltpu.VMEM((2, region.shape[1], 2 * cols * STRIDE), jnp.bfloat16),
            pltpu.VMEM((2, region.shape[1], 2 * cols * STRIDE), jnp.bfloat16),
            pltpu.VMEM((2, count, FREQ, 2 * PATCH), jnp.float32),
            pltpu.VMEM((count, PATCH), jnp.float32),
            pltpu.VMEM((count, PATCH), jnp.float32),
            pltpu.VMEM((count, PATCH), jnp.float32),
        ],
        name="flow",
    )(region, left, right, back)


def shifted(value, axis, by):
    length = lax.axis_size(axis)
    pairs = [(i, i + by) for i in range(length) if 0 <= i + by < length]
    return lax.ppermute(value, axis, pairs)


def padded_2(value, sides, width):
    for axis, dim in sides:
        size, length = (lax.axis_size(axis), value.shape[dim])
        up = [(i, (i + 1) % size) for i in range(size - 1)]
        down = [(j, i) for i, j in up]
        last = lax.slice_in_dim(value, length - width, length, axis=dim)
        first = lax.slice_in_dim(value, 0, width, axis=dim)
        before = lax.ppermute(last, axis, up)
        after = lax.ppermute(first, axis, down)
        value = jnp.concatenate([before, value, after], axis=dim)
    return value


def lap_of(padded, center):
    return (
        padded[:, :-2, 1:-1]
        + padded[:, 2:, 1:-1]
        + padded[:, 1:-1, :-2]
        + padded[:, 1:-1, 2:]
        - 4.0 * center
    )


def whole_sections(images):
    tile = images[0]
    rows, cols = tile.shape[0] // STRIDE, tile.shape[1] // STRIDE
    region = padded_2(jnp.stack([tile, shifted(tile, "sec", -1)]), (("ty", 1), ("tx", 2)), HALF)
    flow = flow_of(region, rows, cols)[:, :cols].reshape(2, rows, cols)
    keep = (lax.axis_index("sec") < lax.axis_size("sec") - 1).astype(jnp.float32)
    flow = flow * keep
    padded = padded_2(flow, (("ty", 1), ("tx", 2)), 2)
    inner = padded[:, 1:-1, 1:-1]
    first = inner + rate * (stiffness * lap_of(padded, inner) + inner - inner)
    row_ids = lax.axis_index("ty") * rows + jnp.arange(-1, rows + 1, dtype=jnp.int32)
    col_ids = lax.axis_index("tx") * cols + jnp.arange(-1, cols + 1, dtype=jnp.int32)
    row_ok = (row_ids >= 0) & (row_ids < rows * lax.axis_size("ty"))
    col_ok = (col_ids >= 0) & (col_ids < cols * lax.axis_size("tx"))
    first = first * (row_ok[:, None] & col_ok[None, :]).astype(jnp.float32)[None]
    center = first[:, 1:-1, 1:-1]
    mesh = center + rate * (stiffness * lap_of(first, center) + flow - center)
    everything = lax.all_gather(mesh, "sec")
    earlier = jnp.arange(lax.axis_size("sec")) < lax.axis_index("sec")
    before = jnp.sum(jnp.where(earlier[:, None, None, None], everything, 0.0), axis=0)
    return (mesh[None], before[None])


AXES = ("sec", "ty", "tx")


def placed(half, y, x):
    ny, nx = lax.axis_size("ty"), lax.axis_size("tx")
    return (((half + x) % 2) * ny + y) * nx + x


def along(value, step):
    ny, nx = lax.axis_size("ty"), lax.axis_size("tx")
    pairs = []
    for y in range(ny):
        for g in range(2 * nx):
            to = step(g) % (2 * nx)
            pairs.append((placed(g % 2, y, g // 2), placed(to % 2, y, to // 2)))
    return lax.ppermute(value, AXES, pairs)


def ring(value, axis, by):
    size = lax.axis_size(axis)
    return lax.ppermute(value, axis, [(i, (i + by) % size) for i in range(size)])


def mate(g):
    return g ^ 1


def near(g):
    return g - 1 if g % 2 == 0 else g + 1


def far(g):
    return g - 2 if g % 2 == 0 else g + 2


def window_kernel(width, place_ref, own_ref, mate_ref, near_ref, far_ref, out_ref):
    half = place_ref[0] == 1
    own, other, close, beyond = own_ref[...], mate_ref[...], near_ref[...], far_ref[...]
    lane = lax.broadcasted_iota(jnp.int32, own.shape, 1)
    begin = jnp.where(half, beyond, close)
    left = jnp.where(half, other, own)
    right = jnp.where(half, own, other)
    end = jnp.where(half, close, beyond)
    begin = jnp.where(place_ref[2] == 0, 0.0, begin)
    end = jnp.where(place_ref[2] == place_ref[4] - 1, 0.0, end)
    begin = pltpu.roll(begin, PATCH + 2 - width, 1)
    left, right, end = pltpu.roll(left, 2, 1), pltpu.roll(right, 2 + width, 1), pltpu.roll(end, 2 + 2 * width, 1)
    value = jnp.where(lane < 2, begin, jnp.where(lane < 2 + width, left, right))
    value = jnp.where(lane < 2 + 2 * width, value, jnp.where(lane < 4 + 2 * width, end, 0.0))
    out_ref[...] = value


def relax_kernel(rows, cols, place_ref, own_ref, above_ref, below_ref, mesh_ref, earlier_ref):
    section, y, x = place_ref[1], place_ref[3], place_ref[2]
    tall = rows + 4
    shape = (tall, PATCH)
    row = lax.broadcasted_iota(jnp.int32, shape, 0) - 2 + y * rows
    col = lax.broadcasted_iota(jnp.int32, shape, 1) - 2 + x * cols
    inside = (row >= 0) & (row < place_ref[5] * rows) & (col >= 0) & (col < place_ref[4] * cols)

    def step(mesh, flow):
        around = (
            pltpu.roll(mesh, 1, 0) + pltpu.roll(mesh, tall - 1, 0)
            + pltpu.roll(mesh, 1, 1) + pltpu.roll(mesh, PATCH - 1, 1)
        )
        lap = around - 4.0 * mesh
        return jnp.where(inside, mesh + rate * (stiffness * lap + flow - mesh), 0.0)

    for c in range(2):
        flow = jnp.concatenate(
            [above_ref[(c + 1) * rows - 2:(c + 1) * rows], own_ref[c * rows:(c + 1) * rows],
             below_ref[c * rows:c * rows + 2]], axis=0)
        flow = jnp.where(inside, flow, 0.0)
        mesh = step(step(flow, flow), flow)
        mesh = pltpu.roll(pltpu.roll(mesh, tall - 2, 0), PATCH - 2, 1)[:rows, :cols]
        mesh_ref[0, c] = jnp.where(section == 0, mesh, 0.0)
        earlier_ref[0, c] = jnp.where(section == 0, 0.0, mesh)


def shared_section(images):
    tile = images[0]
    section, y, x = lax.axis_index("sec"), lax.axis_index("ty"), lax.axis_index("tx")
    ny, nx = lax.axis_size("ty"), lax.axis_size("tx")
    half = (section + x) % 2
    rows, cols = tile.shape[0] // STRIDE, tile.shape[1] // STRIDE
    width = cols // 2
    core = width * STRIDE + HALF
    skip = tile.shape[1] - core
    place = jnp.stack([half, section, x, y, nx * jnp.ones_like(x), ny * jnp.ones_like(x)]).astype(jnp.int32)

    own = lax.dynamic_slice_in_dim(tile, half * skip, core, 1)
    got = along(lax.dynamic_slice_in_dim(tile, (1 - half) * skip, core, 1), mate)
    pair = jnp.stack([jnp.where(section == 0, own, got), jnp.where(section == 0, got, own)])
    above = jnp.where(y > 0, ring(pair[:, -HALF:], "ty", 1), 0.0)
    below = jnp.where(y < ny - 1, ring(pair[:, :HALF], "ty", -1), 0.0)
    pair = jnp.concatenate([above, pair, below], axis=1)
    edge = along(jnp.where(half == 0, pair[:, :, :HALF], pair[:, :, -HALF:]), near)
    at_end = jnp.where(half == 0, x == 0, x == nx - 1)
    edge = jnp.where(at_end, 0.0, edge)
    region = jnp.where(
        half == 0, jnp.concatenate([edge, pair], axis=2), jnp.concatenate([pair, edge], axis=2)
    )
    flow = flow_of(region, rows, width)
    smem, vmem = pl.BlockSpec(memory_space=pltpu.SMEM), pl.BlockSpec(memory_space=pltpu.VMEM)
    window = pl.pallas_call(
        functools.partial(window_kernel, width),
        out_shape=jax.ShapeDtypeStruct(flow.shape, jnp.float32),
        in_specs=[smem] + [vmem] * 4,
        out_specs=vmem,
        name="window",
    )(place, flow, along(flow, mate), along(flow, near), along(flow, far))
    out = jax.ShapeDtypeStruct((1, 2, rows, cols), jnp.float32)
    return pl.pallas_call(
        functools.partial(relax_kernel, rows, cols),
        out_shape=(out, out),
        in_specs=[smem] + [vmem] * 3,
        out_specs=(vmem, vmem),
        name="relax",
    )(place, window, ring(window, "ty", 1), ring(window, "ty", -1))


def solution(mesh):
    in_specs = (P("sec", "ty", "tx"),)
    out_specs = (P("sec", None, "ty", "tx"), P("sec", None, "ty", "tx"))
    shared = mesh.shape["sec"] == 2
    return jax.shard_map(
        shared_section if shared else whole_sections,
        mesh=mesh, in_specs=in_specs, out_specs=out_specs, check_vma=False,
    )
```

time: 138 us -> 57.4 us (0.42)
  matrix products: 68.1 us -> 0 us
  waiting for transfers between devices: 34.4 us -> 24 us
  Pallas kernels: 0 us -> 9.89 us
  other arithmetic: 7.25 us -> 1.64 us
  blocking collectives: 4.36 us -> 0 us
  starting transfers between devices: 18.8 us -> 17.4 us
    dot_general x48 -> x0, matrix products: 68.1 us -> none  [the longest x24 40.4 us: right_apply(): jnp.einsum('snjk,kl->snjl', values, table, precision=lax.Precision.HIGHEST)]
    ppermute x9, waiting for transfers between devices: 34.4 us -> 24 us  [the longest x5 18.4 us: along(): return lax.ppermute(value, AXES, pairs)]
    pallas_call x0 -> x3, Pallas kernels: none -> 9.89 us  [the longest x1 6.79 us: flow_of(): pl.pallas_call(functools.partial(flow_kernel, rows, cols, group), out_sha...]
    all_gather x1 -> x0, blocking collectives: 4.36 us -> none  [prefix(): everything = lax.all_gather(value, axis)]
    reduce_sum x12 -> x0, other arithmetic: 2.87 us -> none  [the longest x4 1.25 us: soft_flow(): flow_y = jnp.sum(weights * offsets[:, None], axis=(1, 2))]
    transpose x1 -> x0, other arithmetic: 1.69 us -> none  [on_device(): bands = jnp.transpose(bands, (1, 0, 2, 3))]
    unnamed x7 -> x12, local copies, waits for them, and re-layouts: 2.73 us -> 1.2 us
    select_n x2 -> x5, other arithmetic: 0.03 us -> 1.46 us  [the longest x1 1.38 us: shared_section(): jnp.where(half == 0, jnp.concatenate([edge, pair], axis=2), jnp.concatena...]
  transfers between devices with their start and end apart: 9 -> 9, of which waited for: 6 -> 7; matrix products, arithmetic and copies ran while one was open for 0% -> 1% of each run, Pallas kernels for 0% -> 0%
where the time goes in v1:
time: 57.4 us; the launch traced here: 56.8 us
  waiting for transfers between devices  24 us (42%)
  starting transfers between devices  17.4 us (30%)
  Pallas kernels  9.89 us (17%)
  local copies, waits for them, and re-layouts  3.1 us (5%)
  other arithmetic  1.64 us (3%)
  between operations  0.74 us (1%)
    ppermute x5, waiting for transfers between devices, along(): return lax.ppermute(value, AXES, pairs)  18.4 us
    ppermute x5, starting transfers between devices, along(): return lax.ppermute(value, AXES, pairs)  15.1 us
    pallas_call x1, Pallas kernels, flow_of(): pl.pallas_call(functools.partial(flow_kernel, rows, cols, group), out_sha...  6.79 us
    ppermute x4, waiting for transfers between devices, ring(): lax.ppermute(value, axis, [(i, (i + by) % size) for i in range(size)])  5.53 us
    ppermute x4, starting transfers between devices, ring(): lax.ppermute(value, axis, [(i, (i + by) % size) for i in range(size)])  2.29 us
    pallas_call x1, Pallas kernels, shared_section(): pl.pallas_call(functools.partial(relax_kernel, rows, cols), out_shape=(ou...  1.63 us
    pallas_call x1, Pallas kernels, shared_section(): pl.pallas_call(functools.partial(window_kernel, width), out_shape=jax.Sha...  1.48 us
    select_n x1, other arithmetic, shared_section(): jnp.where(half == 0, jnp.concatenate([edge, pair], axis=2), jnp.concatena...  1.38 us
  transfers between devices with their start and end apart: 9, of which 7 were waited for; matrix products, arithmetic and copies ran while one was open for 1% of the time, Pallas kernels for 0%

profile of v1, /device:TPU:0, one launch (start us, length us, event | category | flops | bytes accessed | tf_op | source)
XLA Modules:
  0.0 56.8 jit_solution(9412888266511612267)
XLA Ops:
  0.6 0.0 copy-start
  0.7 1.2 %dynamic-slice_bitcast_fusion = f32[256,288]{1,0:T(8,128)S(1)} fusion(f32[1,256,512]{2,1,0:T(8,128)} %param.4, s32[]{:T(128)S(6)} %select_n.75), kind=kLoop, calls=%fused_computation.5 | loop fusion | bytes 589828 | tf_op jit(solution)/shard_map/dynamic_slice | solution.py:288
  1.9 3.1 %collective-permute-start = (f32[256,288]{1,0:T(8,128)S(1)}, f32[256,288]{1,0:T(8,128)S(1)}, u32[]{:S(2)}, u32[]{:S(2)}) collective-permute-start(f32[256,288]{1,0:T(8,128)S(1)} %dynamic-slice_bitcast_fusion), channel_id=1, source_target_pairs={{0,16},{16,0},{17,1},{1,17},{2,18},{18,2},{19,3},{3,19},{4,20},{20... | collective-permute-start | bytes 884744 | tf_op jit(solution)/shard_map/ppermute | solution.py:212
  5.0 9.1 %collective-permute-done = f32[256,288]{1,0:T(8,128)S(1)} collective-permute-done((f32[256,288]{1,0:T(8,128)S(1)}, f32[256,288]{1,0:T(8,128)S(1)}, u32[]{:S(2)}, u32[]{:S(2)}) %collective-permute-start) | collective-permute-done | bytes 294944 | tf_op jit(solution)/shard_map/ppermute | solution.py:212
  14.1 0.0 copy-done
  14.1 0.2 fusion
  14.3 0.1 collective-permute-start.1
  14.4 1.7 %collective-permute-start.2 = (f32[2,32,288]{2,1,0:T(8,128)S(1)}, f32[2,32,288]{2,1,0:T(8,128)S(1)}, u32[]{:S(2)}, u32[]{:S(2)}) collective-permute-start(f32[2,32,288]{2,1,0:T(8,128)S(1)} %get-tuple-element.5), channel_id=1, source_target_pairs={{0,12},{4,0},{8,4},{12,8},{1,13},{5,1},{9,5},{13,9},{2,14},{6,2},{... | collective-permute-start | bytes 221192 | tf_op jit(solution)/shard_map/ppermute | solution.py:217
  16.1 2.3 %collective-permute-done.1 = f32[2,32,288]{2,1,0:T(8,128)S(1)} collective-permute-done((f32[2,32,288]{2,1,0:T(8,128)S(1)}, f32[2,32,288]{2,1,0:T(8,128)S(1)}, u32[]{:S(2)}, u32[]{:S(2)}) %collective-permute-start.1) | collective-permute-done | bytes 73760 | tf_op jit(solution)/shard_map/ppermute | solution.py:217
  18.4 0.2 collective-permute-done.2
  18.7 3.7 %collective-permute-start.3 = (f32[2,320,32]{2,1,0:T(8,128)S(1)}, f32[2,320,32]{2,1,0:T(8,128)S(1)}, u32[]{:S(2)}, u32[]{:S(2)}) collective-permute-start(f32[2,320,32]{2,1,0:T(8,128)S(1)} %fusion.2), channel_id=1, source_target_pairs={{0,3},{16,17},{17,16},{1,2},{2,1},{18,19},{19,18},{3,0},{4,7},{20,... | collective-permute-start | bytes 245768 | tf_op jit(solution)/shard_map/ppermute | solution.py:212
  22.4 8.1 %collective-permute-done.3 = f32[2,320,32]{2,1,0:T(8,128)S(1)} collective-permute-done((f32[2,320,32]{2,1,0:T(8,128)S(1)}, f32[2,320,32]{2,1,0:T(8,128)S(1)}, u32[]{:S(2)}, u32[]{:S(2)}) %collective-permute-start.3) | collective-permute-done | bytes 81952 | tf_op jit(solution)/shard_map/ppermute | solution.py:212
  30.6 1.4 %maximum_select_fusion.region_ref = f32[2,320,320]{2,1,0:T(8,128)} fusion(f32[2,32,288]{2,1,0:T(8,128)S(1)} %broadcast_select_fusion.1, f32[1,256,288]{2,1,0:T(8,128)S(1)} %get-tuple-element.3, f32[1,256,288]{2,1,0:T(8,128)S(1)} %get-tuple-element.2, f32[2,32,288]{2,1,0:T(8,128)S(1)} %broadcast_select_fusion.2, f32[2,320,32]{2,1,0:T(8,128)S(1)} %broadcast_select_fusion, ...), kind=kLoop, calls=%fused_computation | loop fusion | flops 1843200 | bytes 1638401 | tf_op jit(solution)/shard_map/jit(_where)/select_n | solution.py:296
  32.0 6.8 %flow.1.own_ref = f32[8,128]{1,0:T(8,128)} custom-call(f32[2,320,320]{2,1,0:T(8,128)} %maximum_select_fusion.region_ref, bf16[144,384]{1,0:T(8,128)(2,1)} %constant.46.clone.left_ref, bf16[2,256,256]{2,1,0:T(8,128)(2,1)} %constant.47.clone.right_ref, bf16[128,432]{1,0:T(8,128)(2,1)} %constant.48.clone.back_ref), custom_call_target="tpu_custom_call" | custom-call | tf_op jit(solution)/shard_map/flow/pallas_call | solution.py:128
  38.7 2.8 %collective-permute-start.6 = (f32[8,128]{1,0:T(8,128)}, f32[8,128]{1,0:T(8,128)S(1)}, u32[]{:S(2)}, u32[]{:S(2)}) collective-permute-start(f32[8,128]{1,0:T(8,128)} %flow.1.own_ref), channel_id=1, source_target_pairs={{0,19},{16,1},{17,0},{1,18},{2,17},{18,3},{19,2},{3,16},{4,23},{20... | collective-permute-start | bytes 12296 | tf_op jit(solution)/shard_map/ppermute | solution.py:212
  41.5 1.0 %collective-permute-start.5 = (f32[8,128]{1,0:T(8,128)}, f32[8,128]{1,0:T(8,128)S(1)}, u32[]{:S(2)}, u32[]{:S(2)}) collective-permute-start(f32[8,128]{1,0:T(8,128)} %flow.1.own_ref), channel_id=1, source_target_pairs={{0,3},{16,17},{17,16},{1,2},{2,1},{18,19},{19,18},{3,0},{4,7},{20,... | collective-permute-start | bytes 12296 | tf_op jit(solution)/shard_map/ppermute | solution.py:212
  42.5 4.6 %collective-permute-start.4 = (f32[8,128]{1,0:T(8,128)}, f32[8,128]{1,0:T(8,128)S(1)}, u32[]{:S(2)}, u32[]{:S(2)}) collective-permute-start(f32[8,128]{1,0:T(8,128)} %flow.1.own_ref), channel_id=1, source_target_pairs={{0,16},{16,0},{17,1},{1,17},{2,18},{18,2},{19,3},{3,19},{4,20},{20... | collective-permute-start | bytes 12296 | tf_op jit(solution)/shard_map/ppermute | solution.py:212
  47.1 0.7 %stack.28.place_ref = s32[6]{0:T(128)} concatenate(s32[1]{0:T(128)} %bitcast, s32[1]{0:T(128)} %bitcast.1, s32[1]{0:T(128)} %bitcast.2, s32[1]{0:T(128)} %bitcast.3, s32[2]{0:T(128)S(1)} %broadcast.4), dimensions={0} | concatenate | bytes 48 | tf_op jit(solution)/shard_map/stack | solution.py:285
  47.8 0.0 collective-permute-done.6.far_ref
  47.8 0.0 copy-start.3
  47.8 0.0 collective-permute-done.5.near_ref
  47.8 0.0 copy-start.4
  47.8 1.2 %collective-permute-done.4.mate_ref = f32[8,128]{1,0:T(8,128)S(1)} collective-permute-done((f32[8,128]{1,0:T(8,128)}, f32[8,128]{1,0:T(8,128)S(1)}, u32[]{:S(2)}, u32[]{:S(2)}) %collective-permute-start.4) | collective-permute-done | bytes 4128 | tf_op jit(solution)/shard_map/ppermute | solution.py:212
  48.9 0.0 copy-done.3
  48.9 0.0 copy-done.4
  48.9 0.0 copy-start.5
  48.9 0.6 %copy-done.5 = f32[8,128]{1,0:T(8,128)} copy-done((f32[8,128]{1,0:T(8,128)}, f32[8,128]{1,0:T(8,128)S(1)}, u32[]{:S(2)}) %copy-start.5) | copy-done | bytes 4120
  49.5 1.5 %window.1.own_ref = f32[8,128]{1,0:T(8,128)} custom-call(s32[6]{0:T(128)} %stack.28.place_ref, f32[8,128]{1,0:T(8,128)} %flow.1.own_ref, f32[8,128]{1,0:T(8,128)} %copy-done.5, f32[8,128]{1,0:T(8,128)} %copy-done.4, f32[8,128]{1,0:T(8,128)} %copy-done.3), custom_call_target="tpu_custom_call" | custom-call | tf_op jit(solution)/shard_map/window/pallas_call | solution.py:301
  51.0 0.1 collective-permute-start.8
  51.1 0.4 collective-permute-start.7
  51.5 1.2 %collective-permute-done.8.below_ref = f32[8,128]{1,0:T(8,128)S(1)} collective-permute-done((f32[8,128]{1,0:T(8,128)}, f32[8,128]{1,0:T(8,128)S(1)}, u32[]{:S(2)}, u32[]{:S(2)}) %collective-permute-start.8) | collective-permute-done | bytes 4128 | tf_op jit(solution)/shard_map/ppermute | solution.py:217
  52.7 0.0 copy-start.1
  52.7 1.8 %collective-permute-done.7.above_ref = f32[8,128]{1,0:T(8,128)S(1)} collective-permute-done((f32[8,128]{1,0:T(8,128)}, f32[8,128]{1,0:T(8,128)S(1)}, u32[]{:S(2)}, u32[]{:S(2)}) %collective-permute-start.7) | collective-permute-done | bytes 4128 | tf_op jit(solution)/shard_map/ppermute | solution.py:217
  54.5 0.0 copy-done.1
  54.5 0.0 copy-start.2
  54.5 0.6 %copy-done.2 = f32[8,128]{1,0:T(8,128)} copy-done((f32[8,128]{1,0:T(8,128)}, f32[8,128]{1,0:T(8,128)S(1)}, u32[]{:S(2)}) %copy-start.2) | copy-done | bytes 4120
  55.1 1.6 %relax.1 = (f32[1,2,4,8]{3,2,1,0:T(4,128)}, f32[1,2,4,8]{3,2,1,0:T(4,128)}) custom-call(s32[6]{0:T(128)} %stack.28.place_ref, f32[8,128]{1,0:T(8,128)} %window.1.own_ref, f32[8,128]{1,0:T(8,128)} %copy-done.2, f32[8,128]{1,0:T(8,128)} %copy-done.1), custom_call_target="tpu_custom_call" | custom-call | tf_op jit(solution)/shard_map/relax/pallas_call | solution.py:309
  (6 shorter events, 0.1 us)
Async XLA Ops:
  0.6 13.5 %copy-start = (f32[1,256,512]{2,1,0:T(8,128)S(1)}, f32[1,256,512]{2,1,0:T(8,128)}, u32[]{:S(2)}) copy-start(f32[1,256,512]{2,1,0:T(8,128)} %param.4) | copy-start | bytes 1572868
  1.9 12.2 %collective-permute-start = (f32[256,288]{1,0:T(8,128)S(1)}, f32[256,288]{1,0:T(8,128)S(1)}, u32[]{:S(2)}, u32[]{:S(2)}) collective-permute-start(f32[256,288]{1,0:T(8,128)S(1)} %dynamic-slice_bitcast_fusion), channel_id=1, source_target_pairs={{0,16},{16,0},{17,1},{1,17},{2,18},{18,2},{19,3},{3,19},{4,20},{20... | collective-permute-start | bytes 884744 | tf_op jit(solution)/shard_map/ppermute | solution.py:212
  14.3 4.1 %collective-permute-start.1 = (f32[2,32,288]{2,1,0:T(8,128)S(1)}, f32[2,32,288]{2,1,0:T(8,128)S(1)}, u32[]{:S(2)}, u32[]{:S(2)}) collective-permute-start(f32[2,32,288]{2,1,0:T(8,128)S(1)} %get-tuple-element.4), channel_id=1, source_target_pairs={{0,4},{4,8},{8,12},{12,0},{1,5},{5,9},{9,13},{13,1},{2,6},{6,10},{... | collective-permute-start | bytes 221192 | tf_op jit(solution)/shard_map/ppermute | solution.py:217
  14.4 4.3 %collective-permute-start.2 = (f32[2,32,288]{2,1,0:T(8,128)S(1)}, f32[2,32,288]{2,1,0:T(8,128)S(1)}, u32[]{:S(2)}, u32[]{:S(2)}) collective-permute-start(f32[2,32,288]{2,1,0:T(8,128)S(1)} %get-tuple-element.5), channel_id=1, source_target_pairs={{0,12},{4,0},{8,4},{12,8},{1,13},{5,1},{9,5},{13,9},{2,14},{6,2},{... | collective-permute-start | bytes 221192 | tf_op jit(solution)/shard_map/ppermute | solution.py:217
  18.7 11.9 %collective-permute-start.3 = (f32[2,320,32]{2,1,0:T(8,128)S(1)}, f32[2,320,32]{2,1,0:T(8,128)S(1)}, u32[]{:S(2)}, u32[]{:S(2)}) collective-permute-start(f32[2,320,32]{2,1,0:T(8,128)S(1)} %fusion.2), channel_id=1, source_target_pairs={{0,3},{16,17},{17,16},{1,2},{2,1},{18,19},{19,18},{3,0},{4,7},{20,... | collective-permute-start | bytes 245768 | tf_op jit(solution)/shard_map/ppermute | solution.py:212
  38.7 9.0 %collective-permute-start.6 = (f32[8,128]{1,0:T(8,128)}, f32[8,128]{1,0:T(8,128)S(1)}, u32[]{:S(2)}, u32[]{:S(2)}) collective-permute-start(f32[8,128]{1,0:T(8,128)} %flow.1.own_ref), channel_id=1, source_target_pairs={{0,19},{16,1},{17,0},{1,18},{2,17},{18,3},{19,2},{3,16},{4,23},{20... | collective-permute-start | bytes 12296 | tf_op jit(solution)/shard_map/ppermute | solution.py:212
  41.5 6.2 %collective-permute-start.5 = (f32[8,128]{1,0:T(8,128)}, f32[8,128]{1,0:T(8,128)S(1)}, u32[]{:S(2)}, u32[]{:S(2)}) collective-permute-start(f32[8,128]{1,0:T(8,128)} %flow.1.own_ref), channel_id=1, source_target_pairs={{0,3},{16,17},{17,16},{1,2},{2,1},{18,19},{19,18},{3,0},{4,7},{20,... | collective-permute-start | bytes 12296 | tf_op jit(solution)/shard_map/ppermute | solution.py:212
  42.5 6.4 %collective-permute-start.4 = (f32[8,128]{1,0:T(8,128)}, f32[8,128]{1,0:T(8,128)S(1)}, u32[]{:S(2)}, u32[]{:S(2)}) collective-permute-start(f32[8,128]{1,0:T(8,128)} %flow.1.own_ref), channel_id=1, source_target_pairs={{0,16},{16,0},{17,1},{1,17},{2,18},{18,2},{19,3},{3,19},{4,20},{20... | collective-permute-start | bytes 12296 | tf_op jit(solution)/shard_map/ppermute | solution.py:212
  47.8 1.2 %copy-start.3 = (f32[8,128]{1,0:T(8,128)}, f32[8,128]{1,0:T(8,128)S(1)}, u32[]{:S(2)}) copy-start(f32[8,128]{1,0:T(8,128)S(1)} %collective-permute-done.6.far_ref) | copy-start | bytes 12292
  47.8 1.2 %copy-start.4 = (f32[8,128]{1,0:T(8,128)}, f32[8,128]{1,0:T(8,128)S(1)}, u32[]{:S(2)}) copy-start(f32[8,128]{1,0:T(8,128)S(1)} %collective-permute-done.5.near_ref) | copy-start | bytes 12292
  48.9 0.6 %copy-start.5 = (f32[8,128]{1,0:T(8,128)}, f32[8,128]{1,0:T(8,128)S(1)}, u32[]{:S(2)}) copy-start(f32[8,128]{1,0:T(8,128)S(1)} %collective-permute-done.4.mate_ref) | copy-start | bytes 12292
  51.0 1.7 %collective-permute-start.8 = (f32[8,128]{1,0:T(8,128)}, f32[8,128]{1,0:T(8,128)S(1)}, u32[]{:S(2)}, u32[]{:S(2)}) collective-permute-start(f32[8,128]{1,0:T(8,128)} %window.1.own_ref), channel_id=1, source_target_pairs={{0,12},{4,0},{8,4},{12,8},{1,13},{5,1},{9,5},{13,9},{2,14},{6,2},{... | collective-permute-start | bytes 12296 | tf_op jit(solution)/shard_map/ppermute | solution.py:217
  51.1 3.4 %collective-permute-start.7 = (f32[8,128]{1,0:T(8,128)}, f32[8,128]{1,0:T(8,128)S(1)}, u32[]{:S(2)}, u32[]{:S(2)}) collective-permute-start(f32[8,128]{1,0:T(8,128)} %window.1.own_ref), channel_id=1, source_target_pairs={{0,4},{4,8},{8,12},{12,0},{1,5},{5,9},{9,13},{13,1},{2,6},{6,10},{... | collective-permute-start | bytes 12296 | tf_op jit(solution)/shard_map/ppermute | solution.py:217
  52.7 1.8 %copy-start.1 = (f32[8,128]{1,0:T(8,128)}, f32[8,128]{1,0:T(8,128)S(1)}, u32[]{:S(2)}) copy-start(f32[8,128]{1,0:T(8,128)S(1)} %collective-permute-done.8.below_ref) | copy-start | bytes 12292
  54.5 0.6 %copy-start.2 = (f32[8,128]{1,0:T(8,128)}, f32[8,128]{1,0:T(8,128)S(1)}, u32[]{:S(2)}) copy-start(f32[8,128]{1,0:T(8,128)S(1)} %collective-permute-done.7.above_ref) | copy-start | bytes 12292

commit v2 on v1

--- a/solution.py
+++ b/solution.py
@@ -56,15 +56,23 @@
     return mul(high, right_ref[0]) + mul(low, right_ref[0]) + mul(high, right_ref[1])
 
 
+def keep_region(region, z, wide, high_ref, low_ref):
+    even, odd = region[:, :wide], region[:, STRIDE:STRIDE + wide]
+    for part, values in enumerate((even, odd)):
+        high, low = split(values)
+        high_ref[z, :, part * wide:(part + 1) * wide] = high
+        low_ref[z, :, part * wide:(part + 1) * wide] = low
+
+
 def flow_kernel(rows, cols, group, region_ref, left_ref, right_ref, back_ref, flow_ref,
-                high_ref, low_ref, half_ref, peak_ref, mass_ref, tilt_ref):
-    wide = cols * STRIDE
+                high_ref, low_ref, *scratch):
     for z in range(2):
-        even, odd = region_ref[z, :, :wide], region_ref[z, :, STRIDE:STRIDE + wide]
-        for part, values in enumerate((even, odd)):
-            high, low = split(values)
-            high_ref[z, :, part * wide:(part + 1) * wide] = high
-            low_ref[z, :, part * wide:(part + 1) * wide] = low
+        keep_region(region_ref[z], z, cols * STRIDE, high_ref, low_ref)
+    correlate(rows, cols, group, left_ref, right_ref, back_ref, flow_ref, high_ref, low_ref, *scratch)
+
+
+def correlate(rows, cols, group, left_ref, right_ref, back_ref, flow_ref,
+              high_ref, low_ref, half_ref, peak_ref, mass_ref, tilt_ref):
     order = [2 * t for t in range(cols // 2)] + [2 * t + 1 for t in range(cols // 2)]
     for z in range(2):
         for i in range(rows):
@@ -122,24 +130,42 @@
             )
 
 
+def flow_scratch(rows, cols):
+    tall, count = (rows + 1) * STRIDE, rows * cols
+    return [
+        pltpu.VMEM((2, tall, 2 * cols * STRIDE), jnp.bfloat16),
+        pltpu.VMEM((2, tall, 2 * cols * STRIDE), jnp.bfloat16),
+        pltpu.VMEM((2, count, FREQ, 2 * PATCH), jnp.float32),
+        pltpu.VMEM((count, PATCH), jnp.float32),
+        pltpu.VMEM((count, PATCH), jnp.float32),
+        pltpu.VMEM((count, PATCH), jnp.float32),
+    ]
+
+
+IN_VMEM = pl.BlockSpec(memory_space=pltpu.VMEM)
+
+
+def kernel_call(body, outs, *args, scratch=(), name=None):
+    return pl.pallas_call(
+        body,
+        out_shape=outs,
+        in_specs=[IN_VMEM] * len(args),
+        out_specs=jax.tree.map(lambda _: IN_VMEM, outs),
+        scratch_shapes=scratch,
+        name=name,
+    )(*args)
+
+
+def floats(*shape):
+    return jax.ShapeDtypeStruct(shape, jnp.float32)
+
+
 def flow_of(region, rows, cols, group=4):
-    left, right, back = tables()
-    count = rows * cols
-    return pl.pallas_call(
+    return kernel_call(
         functools.partial(flow_kernel, rows, cols, group),
-        out_shape=jax.ShapeDtypeStruct((2 * rows, PATCH), jnp.float32),
-        in_specs=[pl.BlockSpec(memory_space=pltpu.VMEM)] * 4,
-        out_specs=pl.BlockSpec(memory_space=pltpu.VMEM),
-        scratch_shapes=[
-            pltpu.VMEM((2, region.shape[1], 2 * cols * STRIDE), jnp.bfloat16),
-            pltpu.VMEM((2, region.shape[1], 2 * cols * STRIDE), jnp.bfloat16),
-            pltpu.VMEM((2, count, FREQ, 2 * PATCH), jnp.float32),
-            pltpu.VMEM((count, PATCH), jnp.float32),
-            pltpu.VMEM((count, PATCH), jnp.float32),
-            pltpu.VMEM((count, PATCH), jnp.float32),
-        ],
-        name="flow",
-    )(region, left, right, back)
+        floats(2 * rows, PATCH), region, *tables(),
+        scratch=flow_scratch(rows, cols), name="flow",
+    )
 
 
 def shifted(value, axis, by):
@@ -229,30 +255,117 @@
     return g - 2 if g % 2 == 0 else g + 2
 
 
-def window_kernel(width, place_ref, own_ref, mate_ref, near_ref, far_ref, out_ref):
-    half = place_ref[0] == 1
+def past(g):
+    return g + 2 if g % 2 == 0 else g - 2
+
+
+def where_am_i():
+    section, y, x = lax.axis_index("sec"), lax.axis_index("ty"), lax.axis_index("tx")
+    return section, y, x, (section + x) % 2
+
+
+def cut_kernel(core, tile_ref, out_ref):
+    _, _, _, half = where_am_i()
+    width = tile_ref.shape[1]
+
+    @pl.when(half == 0)
+    def _():
+        out_ref[...] = tile_ref[:, width - core:]
+
+    @pl.when(half == 1)
+    def _():
+        out_ref[...] = tile_ref[:, :core]
+
+
+def strips_kernel(tile_ref, first_ref, last_ref):
+    first_ref[...] = tile_ref[:HALF]
+    last_ref[...] = tile_ref[tile_ref.shape[0] - HALF:]
+
+
+def packed(column):
+    quarter = column.shape[0] // 4
+    return jnp.concatenate([column[q * quarter:(q + 1) * quarter] for q in range(4)], axis=1)
+
+
+def unpacked(block):
+    return jnp.concatenate([block[:, q * HALF:(q + 1) * HALF] for q in range(4)], axis=0)
+
+
+def borders_kernel(core, ny, tile_ref, above_ref, below_ref, strips_ref, near_ref, past_ref):
+    _, y, _, half = where_am_i()
+    width = tile_ref.shape[1]
+    above = jnp.where(y == 0, 0.0, above_ref[...])
+    below = jnp.where(y == ny - 1, 0.0, below_ref[...])
+
+    def column(lanes):
+        return packed(jnp.concatenate([above[:, lanes], tile_ref[:, lanes], below[:, lanes]], axis=0))
+
+    start, end = slice(0, HALF), slice(width - HALF, width)
+    first, last = column(start), column(end)
+
+    @pl.when(half == 0)
+    def _():
+        strips_ref[:HALF], strips_ref[HALF:] = above[:, width - core:], below[:, width - core:]
+        near_ref[...], past_ref[...] = first, last
+
+    @pl.when(half == 1)
+    def _():
+        strips_ref[:HALF], strips_ref[HALF:] = above[:, :core], below[:, :core]
+        near_ref[...], past_ref[...] = last, first
+
+
+def shared_kernel(rows, cols, group, ny, nx, tile_ref, above_ref, below_ref, side_ref,
+                  other_ref, strips_ref, other_side_ref, left_ref, right_ref, back_ref, flow_ref,
+                  high_ref, low_ref, *scratch):
+    section, y, x, half = where_am_i()
+    core, width = other_ref.shape[1], tile_ref.shape[1]
+    wide = cols * STRIDE
+    at_end = jnp.where(half == 0, x == 0, x == nx - 1)
+    own_side = jnp.where(at_end, 0.0, unpacked(side_ref[...]))
+    other_side = jnp.where(at_end, 0.0, unpacked(other_side_ref[...]))
+    above = jnp.where(y == 0, 0.0, above_ref[...])
+    below = jnp.where(y == ny - 1, 0.0, below_ref[...])
+    other = jnp.concatenate([strips_ref[:HALF], other_ref[...], strips_ref[HALF:]], axis=0)
+
+    @pl.when(half == 0)
+    def _():
+        own = jnp.concatenate([above[:, :core], tile_ref[:, :core], below[:, :core]], axis=0)
+        keep_region(jnp.concatenate([own_side, own], axis=1), section, wide, high_ref, low_ref)
+        keep_region(jnp.concatenate([other_side, other], axis=1), 1 - section, wide, high_ref, low_ref)
+
+    @pl.when(half == 1)
+    def _():
+        lanes = slice(width - core, width)
+        own = jnp.concatenate([above[:, lanes], tile_ref[:, lanes], below[:, lanes]], axis=0)
+        keep_region(jnp.concatenate([own, own_side], axis=1), section, wide, high_ref, low_ref)
+        keep_region(jnp.concatenate([other, other_side], axis=1), 1 - section, wide, high_ref, low_ref)
+
+    correlate(rows, cols, group, left_ref, right_ref, back_ref, flow_ref, high_ref, low_ref, *scratch)
+
+
+def window_kernel(width, nx, own_ref, mate_ref, near_ref, far_ref, out_ref):
+    _, _, x, place = where_am_i()
+    half = place == 1
     own, other, close, beyond = own_ref[...], mate_ref[...], near_ref[...], far_ref[...]
     lane = lax.broadcasted_iota(jnp.int32, own.shape, 1)
-    begin = jnp.where(half, beyond, close)
+    begin = jnp.where(x == 0, 0.0, jnp.where(half, beyond, close))
     left = jnp.where(half, other, own)
     right = jnp.where(half, own, other)
-    end = jnp.where(half, close, beyond)
-    begin = jnp.where(place_ref[2] == 0, 0.0, begin)
-    end = jnp.where(place_ref[2] == place_ref[4] - 1, 0.0, end)
-    begin = pltpu.roll(begin, PATCH + 2 - width, 1)
-    left, right, end = pltpu.roll(left, 2, 1), pltpu.roll(right, 2 + width, 1), pltpu.roll(end, 2 + 2 * width, 1)
+    end = jnp.where(x == nx - 1, 0.0, jnp.where(half, close, beyond))
+    begin, left = pltpu.roll(begin, PATCH + 2 - width, 1), pltpu.roll(left, 2, 1)
+    right, end = pltpu.roll(right, 2 + width, 1), pltpu.roll(end, 2 + 2 * width, 1)
     value = jnp.where(lane < 2, begin, jnp.where(lane < 2 + width, left, right))
     value = jnp.where(lane < 2 + 2 * width, value, jnp.where(lane < 4 + 2 * width, end, 0.0))
     out_ref[...] = value
 
 
-def relax_kernel(rows, cols, place_ref, own_ref, above_ref, below_ref, mesh_ref, earlier_ref):
-    section, y, x = place_ref[1], place_ref[3], place_ref[2]
+def relax_kernel(rows, cols, ny, nx, own_ref, above_ref, below_ref, mesh_ref, earlier_ref):
+    section, y, x, _ = where_am_i()
     tall = rows + 4
     shape = (tall, PATCH)
     row = lax.broadcasted_iota(jnp.int32, shape, 0) - 2 + y * rows
     col = lax.broadcasted_iota(jnp.int32, shape, 1) - 2 + x * cols
-    inside = (row >= 0) & (row < place_ref[5] * rows) & (col >= 0) & (col < place_ref[4] * cols)
+    inside = (row >= 0) & (row < ny * rows) & (col >= 0) & (col < nx * cols)
 
     def step(mesh, flow):
         around = (
@@ -275,44 +388,37 @@
 
 def shared_section(images):
     tile = images[0]
-    section, y, x = lax.axis_index("sec"), lax.axis_index("ty"), lax.axis_index("tx")
     ny, nx = lax.axis_size("ty"), lax.axis_size("tx")
-    half = (section + x) % 2
     rows, cols = tile.shape[0] // STRIDE, tile.shape[1] // STRIDE
-    width = cols // 2
-    core = width * STRIDE + HALF
-    skip = tile.shape[1] - core
-    place = jnp.stack([half, section, x, y, nx * jnp.ones_like(x), ny * jnp.ones_like(x)]).astype(jnp.int32)
-
-    own = lax.dynamic_slice_in_dim(tile, half * skip, core, 1)
-    got = along(lax.dynamic_slice_in_dim(tile, (1 - half) * skip, core, 1), mate)
-    pair = jnp.stack([jnp.where(section == 0, own, got), jnp.where(section == 0, got, own)])
-    above = jnp.where(y > 0, ring(pair[:, -HALF:], "ty", 1), 0.0)
-    below = jnp.where(y < ny - 1, ring(pair[:, :HALF], "ty", -1), 0.0)
-    pair = jnp.concatenate([above, pair, below], axis=1)
-    edge = along(jnp.where(half == 0, pair[:, :, :HALF], pair[:, :, -HALF:]), near)
-    at_end = jnp.where(half == 0, x == 0, x == nx - 1)
-    edge = jnp.where(at_end, 0.0, edge)
-    region = jnp.where(
-        half == 0, jnp.concatenate([edge, pair], axis=2), jnp.concatenate([pair, edge], axis=2)
-    )
-    flow = flow_of(region, rows, width)
-    smem, vmem = pl.BlockSpec(memory_space=pltpu.SMEM), pl.BlockSpec(memory_space=pltpu.VMEM)
-    window = pl.pallas_call(
-        functools.partial(window_kernel, width),
-        out_shape=jax.ShapeDtypeStruct(flow.shape, jnp.float32),
-        in_specs=[smem] + [vmem] * 4,
-        out_specs=vmem,
-        name="window",
-    )(place, flow, along(flow, mate), along(flow, near), along(flow, far))
-    out = jax.ShapeDtypeStruct((1, 2, rows, cols), jnp.float32)
-    return pl.pallas_call(
-        functools.partial(relax_kernel, rows, cols),
-        out_shape=(out, out),
-        in_specs=[smem] + [vmem] * 3,
-        out_specs=(vmem, vmem),
-        name="relax",
-    )(place, window, ring(window, "ty", 1), ring(window, "ty", -1))
+    half = cols // 2
+    core = half * STRIDE + HALF
+    tall = tile.shape[0] + 2 * HALF
+
+    payload = kernel_call(functools.partial(cut_kernel, core), floats(tile.shape[0], core), tile, name="cut")
+    other = along(payload, mate)
+    strip = floats(HALF, tile.shape[1])
+    first, last = kernel_call(strips_kernel, (strip, strip), tile, name="strips")
+    above, below = ring(last, "ty", 1), ring(first, "ty", -1)
+    edge = floats(tall // 4, 4 * HALF)
+    strips, edge_near, edge_past = kernel_call(
+        functools.partial(borders_kernel, core, ny), (floats(2 * HALF, core), edge, edge),
+        tile, above, below, name="borders",
+    )
+    strips, side, other_side = along(strips, mate), along(edge_near, near), along(edge_past, past)
+    flow = kernel_call(
+        functools.partial(shared_kernel, rows, half, 4, ny, nx), floats(2 * rows, PATCH),
+        tile, above, below, side, other, strips, other_side, *tables(),
+        scratch=flow_scratch(rows, half), name="flow",
+    )
+    window = kernel_call(
+        functools.partial(window_kernel, half, nx), floats(*flow.shape),
+        flow, along(flow, mate), along(flow, near), along(flow, far), name="window",
+    )
+    out = floats(1, 2, rows, cols)
+    return kernel_call(
+        functools.partial(relax_kernel, rows, cols, ny, nx), (out, out),
+        window, ring(window, "ty", 1), ring(window, "ty", -1), name="relax",
+    )
 
 
 def solution(mesh):

time: 57.4 us -> 48.9 us (0.85)
  waiting for transfers between devices: 24 us -> 14.7 us
  Pallas kernels: 9.89 us -> 16.2 us
  starting transfers between devices: 17.4 us -> 12.7 us
  other arithmetic: 1.64 us -> 0 us
  local copies, waits for them, and re-layouts: 3.1 us -> 4.33 us
    ppermute x5 -> x7, waiting for transfers between devices: 18.4 us -> 9.71 us  [along(): return lax.ppermute(value, AXES, pairs)]
    pallas_call x3 -> x6, Pallas kernels: 9.89 us -> 16.2 us  [kernel_call(): pl.pallas_call(body, out_shape=outs, in_specs=[IN_VMEM] * len(args), out_...]
    ppermute x5 -> x7, starting transfers between devices: 15.1 us -> 10.5 us  [along(): return lax.ppermute(value, AXES, pairs)]
    unnamed x12 -> x22, local copies, waits for them, and re-layouts: 1.2 us -> 4.33 us
    select_n x5 -> x0, other arithmetic: 1.46 us -> none  [the longest x1 1.38 us: shared_section(): jnp.where(half == 0, jnp.concatenate([edge, pair], axis=2), jnp.concatena...]
    dynamic_slice x1 -> x0, local copies, waits for them, and re-layouts: 1.22 us -> none  [shared_section(): lax.dynamic_slice_in_dim(tile, (1 - half) * skip, core, 1)]
    another operation x2 -> x0, local copies, waits for them, and re-layouts: 0.68 us -> none  [the longest x1 0.68 us: shared_section(): jnp.stack([half, section, x, y, nx * jnp.ones_like(x), ny * jnp.ones_like...]
    ppermute x4, waiting for transfers between devices: 5.53 us -> 4.95 us  [ring(): lax.ppermute(value, axis, [(i, (i + by) % size) for i in range(size)])]
  transfers between devices with their start and end apart: 9 -> 11, of which waited for: 7 -> 8; matrix products, arithmetic and copies ran while one was open for 1% -> 0% of each run, Pallas kernels for 0% -> 8%
where the time goes in v2:
time: 48.9 us; the launch traced here: 48.6 us
  Pallas kernels  16.2 us (33%)
  waiting for transfers between devices  14.7 us (30%)
  starting transfers between devices  12.7 us (26%)
  local copies, waits for them, and re-layouts  4.33 us (9%)
  between operations  0.67 us (1%)
    pallas_call x6, Pallas kernels, kernel_call(): pl.pallas_call(body, out_shape=outs, in_specs=[IN_VMEM] * len(args), out_...  16.2 us
    ppermute x7, starting transfers between devices, along(): return lax.ppermute(value, AXES, pairs)  10.5 us
    ppermute x7, waiting for transfers between devices, along(): return lax.ppermute(value, AXES, pairs)  9.71 us
    ppermute x4, waiting for transfers between devices, ring(): lax.ppermute(value, axis, [(i, (i + by) % size) for i in range(size)])  4.95 us
    unnamed x22, local copies, waits for them, and re-layouts  4.33 us
    ppermute x4, starting transfers between devices, ring(): lax.ppermute(value, axis, [(i, (i + by) % size) for i in range(size)])  2.26 us
  transfers between devices with their start and end apart: 11, of which 8 were waited for; matrix products, arithmetic and copies ran while one was open for 0% of the time, Pallas kernels for 8%

profile of v2, /device:TPU:0, one launch (start us, length us, event | category | flops | bytes accessed | tf_op | source)
XLA Modules:
  0.0 48.6 jit_solution(14814445964815967575)
XLA Ops:
  0.6 2.0 %cut.1 = f32[256,288]{1,0:T(8,128)} custom-call(f32[256,512]{1,0:T(8,128)} %bitcast.1), custom_call_target="tpu_custom_call" | custom-call | tf_op jit(solution)/shard_map/cut/pallas_call | solution.py:149
  2.6 2.9 %collective-permute-start.3 = (f32[256,288]{1,0:T(8,128)}, f32[256,288]{1,0:T(8,128)S(1)}, u32[]{:S(2)}, u32[]{:S(2)}) collective-permute-start(f32[256,288]{1,0:T(8,128)} %cut.1), channel_id=1, source_target_pairs={{0,16},{16,0},{17,1},{1,17},{2,18},{18,2},{19,3},{3,19},{4,20},{20... | collective-permute-start | bytes 884744 | tf_op jit(solution)/shard_map/ppermute | solution.py:238
  5.4 1.7 %strips.1 = (f32[32,512]{1,0:T(8,128)}, f32[32,512]{1,0:T(8,128)}) custom-call(f32[256,512]{1,0:T(8,128)} %bitcast.2), custom_call_target="tpu_custom_call" | custom-call | tf_op jit(solution)/shard_map/strips/pallas_call | solution.py:149
  7.1 0.0 collective-permute-start
  7.1 1.7 %collective-permute-start.1 = (f32[32,512]{1,0:T(8,128)}, f32[32,512]{1,0:T(8,128)S(1)}, u32[]{:S(2)}, u32[]{:S(2)}) collective-permute-start(f32[32,512]{1,0:T(8,128)} %get-tuple-element.8), channel_id=1, source_target_pairs={{0,12},{4,0},{8,4},{12,8},{1,13},{5,1},{9,5},{13,9},{2,14},{6,2},{... | collective-permute-start | bytes 196616 | tf_op jit(solution)/shard_map/ppermute | solution.py:243
  8.9 2.2 %collective-permute-done.above_ref = f32[32,512]{1,0:T(8,128)S(1)} collective-permute-done((f32[32,512]{1,0:T(8,128)}, f32[32,512]{1,0:T(8,128)S(1)}, u32[]{:S(2)}, u32[]{:S(2)}) %collective-permute-start) | collective-permute-done | bytes 65568 | tf_op jit(solution)/shard_map/ppermute | solution.py:243
  11.0 0.0 copy-start.1
  11.0 0.1 collective-permute-done.1.below_ref
  11.1 0.6 %copy-done.1 = f32[32,512]{1,0:T(8,128)} copy-done((f32[32,512]{1,0:T(8,128)}, f32[32,512]{1,0:T(8,128)S(1)}, u32[]{:S(2)}) %copy-start.1) | copy-done | bytes 65560
  11.7 0.0 copy-start.2
  11.7 0.6 %copy-done.2 = f32[32,512]{1,0:T(8,128)} copy-done((f32[32,512]{1,0:T(8,128)}, f32[32,512]{1,0:T(8,128)S(1)}, u32[]{:S(2)}) %copy-start.2) | copy-done | bytes 65560
  12.3 2.0 %borders.1 = (f32[64,288]{1,0:T(8,128)}, f32[80,128]{1,0:T(8,128)}, f32[80,128]{1,0:T(8,128)}) custom-call(f32[256,512]{1,0:T(8,128)} %bitcast.3, f32[32,512]{1,0:T(8,128)} %copy-done.1, f32[32,512]{1,0:T(8,128)} %copy-done.2), custom_call_target="tpu_custom_call" | custom-call | tf_op jit(solution)/shard_map/borders/pallas_call | solution.py:149
  14.2 0.0 collective-permute-start.4
  14.2 4.1 %collective-permute-start.2 = (f32[80,128]{1,0:T(8,128)}, f32[80,128]{1,0:T(8,128)S(1)}, u32[]{:S(2)}, u32[]{:S(2)}) collective-permute-start(f32[80,128]{1,0:T(8,128)} %get-tuple-element.9), channel_id=1, source_target_pairs={{0,3},{16,17},{17,16},{1,2},{2,1},{18,19},{19,18},{3,0},{4,7},{20,... | collective-permute-start | bytes 122888 | tf_op jit(solution)/shard_map/ppermute | solution.py:238
  18.4 0.0 collective-permute-start.5
  18.4 2.4 %collective-permute-done.2.side_ref = f32[80,128]{1,0:T(8,128)S(1)} collective-permute-done((f32[80,128]{1,0:T(8,128)}, f32[80,128]{1,0:T(8,128)S(1)}, u32[]{:S(2)}, u32[]{:S(2)}) %collective-permute-start.2) | collective-permute-done | bytes 40992 | tf_op jit(solution)/shard_map/ppermute | solution.py:238
  20.7 0.0 copy-start.4
  20.8 4.7 %collective-permute-done.5.other_side_ref = f32[80,128]{1,0:T(8,128)S(1)} collective-permute-done((f32[80,128]{1,0:T(8,128)}, f32[80,128]{1,0:T(8,128)S(1)}, u32[]{:S(2)}, u32[]{:S(2)}) %collective-permute-start.5) | collective-permute-done | bytes 40992 | tf_op jit(solution)/shard_map/ppermute | solution.py:238
  25.5 0.0 copy-start.5
  25.5 0.0 collective-permute-done.4.strips_ref
  25.5 0.0 copy-start.3
  25.5 0.0 collective-permute-done.3.other_ref
  25.5 0.0 copy-done.4
  25.5 0.6 %copy-done.5 = f32[80,128]{1,0:T(8,128)} copy-done((f32[80,128]{1,0:T(8,128)}, f32[80,128]{1,0:T(8,128)S(1)}, u32[]{:S(2)}) %copy-start.5) | copy-done | bytes 40984
  26.1 0.0 copy-done.3
  26.1 0.0 copy-start
  26.1 0.7 %copy-done = f32[256,288]{1,0:T(8,128)} copy-done((f32[256,288]{1,0:T(8,128)}, f32[256,288]{1,0:T(8,128)S(1)}, u32[]{:S(2)}) %copy-start) | copy-done | bytes 294936
  26.9 7.7 %flow.1.own_ref = f32[8,128]{1,0:T(8,128)} custom-call(f32[256,512]{1,0:T(8,128)} %bitcast.4, f32[32,512]{1,0:T(8,128)} %copy-done.1, f32[32,512]{1,0:T(8,128)} %copy-done.2, f32[80,128]{1,0:T(8,128)} %copy-done.4, f32[256,288]{1,0:T(8,128)} %copy-done, f32[64,288]{1,0:T(8,128)} %copy-done.3, f32[80,128]{1,0:T(8,128)} %copy-done.5, ...), custom_call_target="tpu_custom_call" | custom-call | tf_op jit(solution)/shard_map/flow/pallas_call | solution.py:149
  34.6 0.5 collective-permute-start.8
  35.1 0.8 %collective-permute-start.7 = (f32[8,128]{1,0:T(8,128)}, f32[8,128]{1,0:T(8,128)S(1)}, u32[]{:S(2)}, u32[]{:S(2)}) collective-permute-start(f32[8,128]{1,0:T(8,128)} %flow.1.own_ref), channel_id=1, source_target_pairs={{0,3},{16,17},{17,16},{1,2},{2,1},{18,19},{19,18},{3,0},{4,7},{20,... | collective-permute-start | bytes 12296 | tf_op jit(solution)/shard_map/ppermute | solution.py:238
  35.8 2.2 %collective-permute-start.6 = (f32[8,128]{1,0:T(8,128)}, f32[8,128]{1,0:T(8,128)S(1)}, u32[]{:S(2)}, u32[]{:S(2)}) collective-permute-start(f32[8,128]{1,0:T(8,128)} %flow.1.own_ref), channel_id=1, source_target_pairs={{0,16},{16,0},{17,1},{1,17},{2,18},{18,2},{19,3},{3,19},{4,20},{20... | collective-permute-start | bytes 12296 | tf_op jit(solution)/shard_map/ppermute | solution.py:238
  38.1 1.2 %collective-permute-done.8.far_ref = f32[8,128]{1,0:T(8,128)S(1)} collective-permute-done((f32[8,128]{1,0:T(8,128)}, f32[8,128]{1,0:T(8,128)S(1)}, u32[]{:S(2)}, u32[]{:S(2)}) %collective-permute-start.8) | collective-permute-done | bytes 4128 | tf_op jit(solution)/shard_map/ppermute | solution.py:238
  39.3 0.0 copy-start.6
  39.3 1.4 %collective-permute-done.7.near_ref = f32[8,128]{1,0:T(8,128)S(1)} collective-permute-done((f32[8,128]{1,0:T(8,128)}, f32[8,128]{1,0:T(8,128)S(1)}, u32[]{:S(2)}, u32[]{:S(2)}) %collective-permute-start.7) | collective-permute-done | bytes 4128 | tf_op jit(solution)/shard_map/ppermute | solution.py:238
  40.7 0.0 copy-start.7
  40.7 0.0 collective-permute-done.6.mate_ref
  40.7 0.0 copy-done.6
  40.7 0.6 %copy-done.7 = f32[8,128]{1,0:T(8,128)} copy-done((f32[8,128]{1,0:T(8,128)}, f32[8,128]{1,0:T(8,128)S(1)}, u32[]{:S(2)}) %copy-start.7) | copy-done | bytes 4120
  41.3 0.0 copy-start.9
  41.3 0.6 %copy-done.9 = f32[8,128]{1,0:T(8,128)} copy-done((f32[8,128]{1,0:T(8,128)}, f32[8,128]{1,0:T(8,128)S(1)}, u32[]{:S(2)}) %copy-start.9) | copy-done | bytes 4120
  41.9 1.4 %window.1.own_ref = f32[8,128]{1,0:T(8,128)} custom-call(f32[8,128]{1,0:T(8,128)} %flow.1.own_ref, f32[8,128]{1,0:T(8,128)} %copy-done.9, f32[8,128]{1,0:T(8,128)} %copy-done.7, f32[8,128]{1,0:T(8,128)} %copy-done.6), custom_call_target="tpu_custom_call" | custom-call | tf_op jit(solution)/shard_map/window/pallas_call | solution.py:149
  43.2 0.0 collective-permute-start.10
  43.3 0.5 %collective-permute-start.9 = (f32[8,128]{1,0:T(8,128)}, f32[8,128]{1,0:T(8,128)S(1)}, u32[]{:S(2)}, u32[]{:S(2)}) collective-permute-start(f32[8,128]{1,0:T(8,128)} %window.1.own_ref), channel_id=1, source_target_pairs={{0,4},{4,8},{8,12},{12,0},{1,5},{5,9},{9,13},{13,1},{2,6},{6,10},{... | collective-permute-start | bytes 12296 | tf_op jit(solution)/shard_map/ppermute | solution.py:243
  43.8 1.0 %collective-permute-done.10.below_ref = f32[8,128]{1,0:T(8,128)S(1)} collective-permute-done((f32[8,128]{1,0:T(8,128)}, f32[8,128]{1,0:T(8,128)S(1)}, u32[]{:S(2)}, u32[]{:S(2)}) %collective-permute-start.10) | collective-permute-done | bytes 4128 | tf_op jit(solution)/shard_map/ppermute | solution.py:243
  44.8 1.7 %collective-permute-done.9.above_ref = f32[8,128]{1,0:T(8,128)S(1)} collective-permute-done((f32[8,128]{1,0:T(8,128)}, f32[8,128]{1,0:T(8,128)S(1)}, u32[]{:S(2)}, u32[]{:S(2)}) %collective-permute-start.9) | collective-permute-done | bytes 4128 | tf_op jit(solution)/shard_map/ppermute | solution.py:243
  46.5 0.0 copy-done.8
  46.5 0.6 %copy-done.10 = f32[8,128]{1,0:T(8,128)} copy-done((f32[8,128]{1,0:T(8,128)}, f32[8,128]{1,0:T(8,128)S(1)}, u32[]{:S(2)}) %copy-start.10) | copy-done | bytes 4120
  47.1 1.5 %relax.1 = (f32[1,2,4,8]{3,2,1,0:T(4,128)}, f32[1,2,4,8]{3,2,1,0:T(4,128)}) custom-call(f32[8,128]{1,0:T(8,128)} %window.1.own_ref, f32[8,128]{1,0:T(8,128)} %copy-done.10, f32[8,128]{1,0:T(8,128)} %copy-done.8), custom_call_target="tpu_custom_call" | custom-call | tf_op jit(solution)/shard_map/relax/pallas_call | solution.py:149
  (2 shorter events, 0.0 us)
Async XLA Ops:
  2.6 22.9 %collective-permute-start.3 = (f32[256,288]{1,0:T(8,128)}, f32[256,288]{1,0:T(8,128)S(1)}, u32[]{:S(2)}, u32[]{:S(2)}) collective-permute-start(f32[256,288]{1,0:T(8,128)} %cut.1), channel_id=1, source_target_pairs={{0,16},{16,0},{17,1},{1,17},{2,18},{18,2},{19,3},{3,19},{4,20},{20... | collective-permute-start | bytes 884744 | tf_op jit(solution)/shard_map/ppermute | solution.py:238
  7.1 3.9 %collective-permute-start = (f32[32,512]{1,0:T(8,128)}, f32[32,512]{1,0:T(8,128)S(1)}, u32[]{:S(2)}, u32[]{:S(2)}) collective-permute-start(f32[32,512]{1,0:T(8,128)} %get-tuple-element.7), channel_id=1, source_target_pairs={{0,4},{4,8},{8,12},{12,0},{1,5},{5,9},{9,13},{13,1},{2,6},{6,10},{... | collective-permute-start | bytes 196616 | tf_op jit(solution)/shard_map/ppermute | solution.py:243
  7.1 4.0 %collective-permute-start.1 = (f32[32,512]{1,0:T(8,128)}, f32[32,512]{1,0:T(8,128)S(1)}, u32[]{:S(2)}, u32[]{:S(2)}) collective-permute-start(f32[32,512]{1,0:T(8,128)} %get-tuple-element.8), channel_id=1, source_target_pairs={{0,12},{4,0},{8,4},{12,8},{1,13},{5,1},{9,5},{13,9},{2,14},{6,2},{... | collective-permute-start | bytes 196616 | tf_op jit(solution)/shard_map/ppermute | solution.py:243
  11.0 0.6 %copy-start.1 = (f32[32,512]{1,0:T(8,128)}, f32[32,512]{1,0:T(8,128)S(1)}, u32[]{:S(2)}) copy-start(f32[32,512]{1,0:T(8,128)S(1)} %collective-permute-done.above_ref) | copy-start | bytes 196612
  11.7 0.6 %copy-start.2 = (f32[32,512]{1,0:T(8,128)}, f32[32,512]{1,0:T(8,128)S(1)}, u32[]{:S(2)}) copy-start(f32[32,512]{1,0:T(8,128)S(1)} %collective-permute-done.1.below_ref) | copy-start | bytes 196612
  14.2 11.2 %collective-permute-start.4 = (f32[64,288]{1,0:T(8,128)}, f32[64,288]{1,0:T(8,128)S(1)}, u32[]{:S(2)}, u32[]{:S(2)}) collective-permute-start(f32[64,288]{1,0:T(8,128)} %get-tuple-element.10), channel_id=1, source_target_pairs={{0,16},{16,0},{17,1},{1,17},{2,18},{18,2},{19,3},{3,19},{4,20},{20... | collective-permute-start | bytes 221192 | tf_op jit(solution)/shard_map/ppermute | solution.py:238
  14.2 6.5 %collective-permute-start.2 = (f32[80,128]{1,0:T(8,128)}, f32[80,128]{1,0:T(8,128)S(1)}, u32[]{:S(2)}, u32[]{:S(2)}) collective-permute-start(f32[80,128]{1,0:T(8,128)} %get-tuple-element.9), channel_id=1, source_target_pairs={{0,3},{16,17},{17,16},{1,2},{2,1},{18,19},{19,18},{3,0},{4,7},{20,... | collective-permute-start | bytes 122888 | tf_op jit(solution)/shard_map/ppermute | solution.py:238
  18.4 7.1 %collective-permute-start.5 = (f32[80,128]{1,0:T(8,128)}, f32[80,128]{1,0:T(8,128)S(1)}, u32[]{:S(2)}, u32[]{:S(2)}) collective-permute-start(f32[80,128]{1,0:T(8,128)} %get-tuple-element.11), channel_id=1, source_target_pairs={{0,17},{16,3},{17,2},{1,16},{2,19},{18,1},{19,0},{3,18},{4,21},{20... | collective-permute-start | bytes 122888 | tf_op jit(solution)/shard_map/ppermute | solution.py:238
  20.7 4.7 %copy-start.4 = (f32[80,128]{1,0:T(8,128)}, f32[80,128]{1,0:T(8,128)S(1)}, u32[]{:S(2)}) copy-start(f32[80,128]{1,0:T(8,128)S(1)} %collective-permute-done.2.side_ref) | copy-start | bytes 122884
  25.5 0.6 %copy-start.5 = (f32[80,128]{1,0:T(8,128)}, f32[80,128]{1,0:T(8,128)S(1)}, u32[]{:S(2)}) copy-start(f32[80,128]{1,0:T(8,128)S(1)} %collective-permute-done.5.other_side_ref) | copy-start | bytes 122884
  25.5 0.6 %copy-start.3 = (f32[64,288]{1,0:T(8,128)}, f32[64,288]{1,0:T(8,128)S(1)}, u32[]{:S(2)}) copy-start(f32[64,288]{1,0:T(8,128)S(1)} %collective-permute-done.4.strips_ref) | copy-start | bytes 221188
  26.1 0.7 %copy-start = (f32[256,288]{1,0:T(8,128)}, f32[256,288]{1,0:T(8,128)S(1)}, u32[]{:S(2)}) copy-start(f32[256,288]{1,0:T(8,128)S(1)} %collective-permute-done.3.other_ref) | copy-start | bytes 884740
  34.6 4.7 %collective-permute-start.8 = (f32[8,128]{1,0:T(8,128)}, f32[8,128]{1,0:T(8,128)S(1)}, u32[]{:S(2)}, u32[]{:S(2)}) collective-permute-start(f32[8,128]{1,0:T(8,128)} %flow.1.own_ref), channel_id=1, source_target_pairs={{0,19},{16,1},{17,0},{1,18},{2,17},{18,3},{19,2},{3,16},{4,23},{20... | collective-permute-start | bytes 12296 | tf_op jit(solution)/shard_map/ppermute | solution.py:238
  35.1 5.6 %collective-permute-start.7 = (f32[8,128]{1,0:T(8,128)}, f32[8,128]{1,0:T(8,128)S(1)}, u32[]{:S(2)}, u32[]{:S(2)}) collective-permute-start(f32[8,128]{1,0:T(8,128)} %flow.1.own_ref), channel_id=1, source_target_pairs={{0,3},{16,17},{17,16},{1,2},{2,1},{18,19},{19,18},{3,0},{4,7},{20,... | collective-permute-start | bytes 12296 | tf_op jit(solution)/shard_map/ppermute | solution.py:238
  35.8 4.9 %collective-permute-start.6 = (f32[8,128]{1,0:T(8,128)}, f32[8,128]{1,0:T(8,128)S(1)}, u32[]{:S(2)}, u32[]{:S(2)}) collective-permute-start(f32[8,128]{1,0:T(8,128)} %flow.1.own_ref), channel_id=1, source_target_pairs={{0,16},{16,0},{17,1},{1,17},{2,18},{18,2},{19,3},{3,19},{4,20},{20... | collective-permute-start | bytes 12296 | tf_op jit(solution)/shard_map/ppermute | solution.py:238
  39.3 1.4 %copy-start.6 = (f32[8,128]{1,0:T(8,128)}, f32[8,128]{1,0:T(8,128)S(1)}, u32[]{:S(2)}) copy-start(f32[8,128]{1,0:T(8,128)S(1)} %collective-permute-done.8.far_ref) | copy-start | bytes 12292
  40.7 0.6 %copy-start.7 = (f32[8,128]{1,0:T(8,128)}, f32[8,128]{1,0:T(8,128)S(1)}, u32[]{:S(2)}) copy-start(f32[8,128]{1,0:T(8,128)S(1)} %collective-permute-done.7.near_ref) | copy-start | bytes 12292
  41.3 0.6 %copy-start.9 = (f32[8,128]{1,0:T(8,128)}, f32[8,128]{1,0:T(8,128)S(1)}, u32[]{:S(2)}) copy-start(f32[8,128]{1,0:T(8,128)S(1)} %collective-permute-done.6.mate_ref) | copy-start | bytes 12292
  43.2 1.5 %collective-permute-start.10 = (f32[8,128]{1,0:T(8,128)}, f32[8,128]{1,0:T(8,128)S(1)}, u32[]{:S(2)}, u32[]{:S(2)}) collective-permute-start(f32[8,128]{1,0:T(8,128)} %window.1.own_ref), channel_id=1, source_target_pairs={{0,12},{4,0},{8,4},{12,8},{1,13},{5,1},{9,5},{13,9},{2,14},{6,2},{... | collective-permute-start | bytes 12296 | tf_op jit(solution)/shard_map/ppermute | solution.py:243
  43.3 3.2 %collective-permute-start.9 = (f32[8,128]{1,0:T(8,128)}, f32[8,128]{1,0:T(8,128)S(1)}, u32[]{:S(2)}, u32[]{:S(2)}) collective-permute-start(f32[8,128]{1,0:T(8,128)} %window.1.own_ref), channel_id=1, source_target_pairs={{0,4},{4,8},{8,12},{12,0},{1,5},{5,9},{9,13},{13,1},{2,6},{6,10},{... | collective-permute-start | bytes 12296 | tf_op jit(solution)/shard_map/ppermute | solution.py:243
  44.8 1.7 %copy-start.8 = (f32[8,128]{1,0:T(8,128)}, f32[8,128]{1,0:T(8,128)S(1)}, u32[]{:S(2)}) copy-start(f32[8,128]{1,0:T(8,128)S(1)} %collective-permute-done.10.below_ref) | copy-start | bytes 12292
  46.5 0.6 %copy-start.10 = (f32[8,128]{1,0:T(8,128)}, f32[8,128]{1,0:T(8,128)S(1)}, u32[]{:S(2)}) copy-start(f32[8,128]{1,0:T(8,128)S(1)} %collective-permute-done.9.above_ref) | copy-start | bytes 12292

commit v3 on v2

--- a/solution.py
+++ b/solution.py
@@ -145,13 +145,16 @@
 IN_VMEM = pl.BlockSpec(memory_space=pltpu.VMEM)
 
 
-def kernel_call(body, outs, *args, scratch=(), name=None):
+def kernel_call(body, outs, *args, scratch=(), name=None, last=False):
+    args = [pltpu.with_memory_space_constraint(a, pltpu.VMEM) if isinstance(a, jax.Array) else a for a in args]
+    shapes = outs if last else jax.tree.map(lambda out: pltpu.VMEM(out.shape, out.dtype), outs)
     return pl.pallas_call(
         body,
-        out_shape=outs,
+        out_shape=shapes,
         in_specs=[IN_VMEM] * len(args),
         out_specs=jax.tree.map(lambda _: IN_VMEM, outs),
         scratch_shapes=scratch,
+        compiler_params=pltpu.CompilerParams(vmem_limit_bytes=24 << 20),
         name=name,
     )(*args)
 
@@ -417,7 +420,7 @@
     out = floats(1, 2, rows, cols)
     return kernel_call(
         functools.partial(relax_kernel, rows, cols, ny, nx), (out, out),
-        window, ring(window, "ty", 1), ring(window, "ty", -1), name="relax",
+        window, ring(window, "ty", 1), ring(window, "ty", -1), name="relax", last=True,
     )
 
 

time: 48.9 us -> 37.1 us (0.76)
  Pallas kernels: 16.2 us -> 6.95 us
  local copies, waits for them, and re-layouts: 4.33 us -> 1.06 us
  waiting for transfers between devices: 14.7 us -> 15.3 us
    pallas_call x6, Pallas kernels: 16.2 us -> 6.95 us  [kernel_call(): pl.pallas_call(body, out_shape=shapes, in_specs=[IN_VMEM] * len(args), ou...]
    unnamed x22 -> x8, local copies, waits for them, and re-layouts: 4.33 us -> 1.06 us
    ppermute x7, waiting for transfers between devices: 9.71 us -> 10.8 us  [along(): return lax.ppermute(value, AXES, pairs)]
  transfers between devices with their start and end apart: 11 -> 11, of which waited for: 8 -> 7; matrix products, arithmetic and copies ran while one was open for 0% -> 0% of each run, Pallas kernels for 8% -> 1%
where the time goes in v3:
time: 37.1 us; the launch traced here: 36.9 us
  waiting for transfers between devices  15.3 us (41%)
  starting transfers between devices  12.9 us (35%)
  Pallas kernels  6.95 us (19%)
  local copies, waits for them, and re-layouts  1.06 us (3%)
  between operations  0.72 us (2%)
    ppermute x7, waiting for transfers between devices, along(): return lax.ppermute(value, AXES, pairs)  10.8 us
    ppermute x7, starting transfers between devices, along(): return lax.ppermute(value, AXES, pairs)  10.6 us
    pallas_call x6, Pallas kernels, kernel_call(): pl.pallas_call(body, out_shape=shapes, in_specs=[IN_VMEM] * len(args), ou...  6.95 us
    ppermute x4, waiting for transfers between devices, ring(): lax.ppermute(value, axis, [(i, (i + by) % size) for i in range(size)])  4.55 us
    ppermute x4, starting transfers between devices, ring(): lax.ppermute(value, axis, [(i, (i + by) % size) for i in range(size)])  2.27 us
    unnamed x8, local copies, waits for them, and re-layouts  1.06 us
  transfers between devices with their start and end apart: 11, of which 7 were waited for; matrix products, arithmetic and copies ran while one was open for 0% of the time, Pallas kernels for 1%

profile of v3, /device:TPU:0, one launch (start us, length us, event | category | flops | bytes accessed | tf_op | source)
XLA Modules:
  0.0 36.9 jit_solution(2575021022846966701)
XLA Ops:
  0.6 0.0 copy-start
  0.6 1.0 %copy-done = f32[1,256,512]{2,1,0:T(8,128)S(1)} copy-done((f32[1,256,512]{2,1,0:T(8,128)S(1)}, f32[1,256,512]{2,1,0:T(8,128)}, u32[]{:S(2)}) %copy-start) | copy-done | bytes 524312
  1.7 0.2 cut.1
  1.8 2.9 %collective-permute-start.3 = (f32[256,288]{1,0:T(8,128)S(1)}, f32[256,288]{1,0:T(8,128)S(1)}, u32[]{:S(2)}, u32[]{:S(2)}) collective-permute-start(f32[256,288]{1,0:T(8,128)S(1)} %cut.1), channel_id=1, source_target_pairs={{0,16},{16,0},{17,1},{1,17},{2,18},{18,2},{19,3},{3,19},{4,20},{20... | collective-permute-start | bytes 884744 | tf_op jit(solution)/shard_map/ppermute | solution.py:241
  4.8 0.1 collective-permute-start
  4.8 0.0 copy-start.1
  4.9 0.0 copy-start.2
  4.9 0.0 copy-start.3
  4.9 1.7 %collective-permute-start.1 = (f32[32,512]{1,0:T(8,128)S(1)}, f32[32,512]{1,0:T(8,128)S(1)}, u32[]{:S(2)}, u32[]{:S(2)}) collective-permute-start(f32[32,512]{1,0:T(8,128)S(1)} %get-tuple-element.8), channel_id=1, source_target_pairs={{0,12},{4,0},{8,4},{12,8},{1,13},{5,1},{9,5},{13,9},{2,14},{6,2},{... | collective-permute-start | bytes 196616 | tf_op jit(solution)/shard_map/ppermute | solution.py:246
  6.6 1.9 %collective-permute-done.above_ref = f32[32,512]{1,0:T(8,128)S(1)} collective-permute-done((f32[32,512]{1,0:T(8,128)S(1)}, f32[32,512]{1,0:T(8,128)S(1)}, u32[]{:S(2)}, u32[]{:S(2)}) %collective-permute-start) | collective-permute-done | bytes 65568 | tf_op jit(solution)/shard_map/ppermute | solution.py:246
  8.5 0.0 collective-permute-done.1.below_ref
  8.5 0.2 borders.1
  8.7 0.4 collective-permute-start.4
  9.1 3.8 %collective-permute-start.2 = (f32[80,128]{1,0:T(8,128)S(1)}, f32[80,128]{1,0:T(8,128)S(1)}, u32[]{:S(2)}, u32[]{:S(2)}) collective-permute-start(f32[80,128]{1,0:T(8,128)S(1)} %get-tuple-element.9), channel_id=1, source_target_pairs={{0,3},{16,17},{17,16},{1,2},{2,1},{18,19},{19,18},{3,0},{4,7},{20,... | collective-permute-start | bytes 122888 | tf_op jit(solution)/shard_map/ppermute | solution.py:241
  12.9 0.0 collective-permute-start.5
  12.9 2.0 %collective-permute-done.2.side_ref = f32[80,128]{1,0:T(8,128)S(1)} collective-permute-done((f32[80,128]{1,0:T(8,128)S(1)}, f32[80,128]{1,0:T(8,128)S(1)}, u32[]{:S(2)}, u32[]{:S(2)}) %collective-permute-start.2) | collective-permute-done | bytes 40992 | tf_op jit(solution)/shard_map/ppermute | solution.py:241
  14.9 4.7 %collective-permute-done.5.other_side_ref = f32[80,128]{1,0:T(8,128)S(1)} collective-permute-done((f32[80,128]{1,0:T(8,128)S(1)}, f32[80,128]{1,0:T(8,128)S(1)}, u32[]{:S(2)}, u32[]{:S(2)}) %collective-permute-start.5) | collective-permute-done | bytes 40992 | tf_op jit(solution)/shard_map/ppermute | solution.py:241
  19.7 0.0 collective-permute-done.4.strips_ref
  19.7 0.0 collective-permute-done.3.other_ref
  19.7 0.0 copy-done.1
  19.7 0.0 copy-done.2
  19.7 0.0 copy-done.3
  19.7 5.7 %flow.1.own_ref = f32[8,128]{1,0:T(8,128)S(1)} custom-call(f32[256,512]{1,0:T(8,128)S(1)} %bitcast.4, f32[32,512]{1,0:T(8,128)S(1)} %collective-permute-done.above_ref, f32[32,512]{1,0:T(8,128)S(1)} %collective-permute-done.1.below_ref, f32[80,128]{1,0:T(8,128)S(1)} %collective-permute-done.2.side_ref, f32[256,288]{1,0:T(8,128)S(1)} %collective-permute-done.3.other_ref, ...), custom_call_target="tpu_custom_call" | custom-call | tf_op jit(solution)/shard_map/flow/pallas_call | solution.py:151
  25.4 2.1 %collective-permute-start.8 = (f32[8,128]{1,0:T(8,128)S(1)}, f32[8,128]{1,0:T(8,128)S(1)}, u32[]{:S(2)}, u32[]{:S(2)}) collective-permute-start(f32[8,128]{1,0:T(8,128)S(1)} %flow.1.own_ref), channel_id=1, source_target_pairs={{0,19},{16,1},{17,0},{1,18},{2,17},{18,3},{19,2},{3,16},{4,23},{20... | collective-permute-start | bytes 12296 | tf_op jit(solution)/shard_map/ppermute | solution.py:241
  27.5 0.1 collective-permute-start.7
  27.6 1.3 %collective-permute-start.6 = (f32[8,128]{1,0:T(8,128)S(1)}, f32[8,128]{1,0:T(8,128)S(1)}, u32[]{:S(2)}, u32[]{:S(2)}) collective-permute-start(f32[8,128]{1,0:T(8,128)S(1)} %flow.1.own_ref), channel_id=1, source_target_pairs={{0,16},{16,0},{17,1},{1,17},{2,18},{18,2},{19,3},{3,19},{4,20},{20... | collective-permute-start | bytes 12296 | tf_op jit(solution)/shard_map/ppermute | solution.py:241
  28.9 1.0 %collective-permute-done.8.far_ref = f32[8,128]{1,0:T(8,128)S(1)} collective-permute-done((f32[8,128]{1,0:T(8,128)S(1)}, f32[8,128]{1,0:T(8,128)S(1)}, u32[]{:S(2)}, u32[]{:S(2)}) %collective-permute-start.8) | collective-permute-done | bytes 4128 | tf_op jit(solution)/shard_map/ppermute | solution.py:241
  29.9 3.0 %collective-permute-done.7.near_ref = f32[8,128]{1,0:T(8,128)S(1)} collective-permute-done((f32[8,128]{1,0:T(8,128)S(1)}, f32[8,128]{1,0:T(8,128)S(1)}, u32[]{:S(2)}, u32[]{:S(2)}) %collective-permute-start.7) | collective-permute-done | bytes 4128 | tf_op jit(solution)/shard_map/ppermute | solution.py:241
  32.9 0.0 collective-permute-done.6.mate_ref
  32.9 0.1 window.1.own_ref
  33.0 0.0 collective-permute-start.10
  33.0 0.5 %collective-permute-start.9 = (f32[8,128]{1,0:T(8,128)S(1)}, f32[8,128]{1,0:T(8,128)S(1)}, u32[]{:S(2)}, u32[]{:S(2)}) collective-permute-start(f32[8,128]{1,0:T(8,128)S(1)} %window.1.own_ref), channel_id=1, source_target_pairs={{0,4},{4,8},{8,12},{12,0},{1,5},{5,9},{9,13},{13,1},{2,6},{6,10},{... | collective-permute-start | bytes 12296 | tf_op jit(solution)/shard_map/ppermute | solution.py:246
  33.5 0.8 %collective-permute-done.10.below_ref = f32[8,128]{1,0:T(8,128)S(1)} collective-permute-done((f32[8,128]{1,0:T(8,128)S(1)}, f32[8,128]{1,0:T(8,128)S(1)}, u32[]{:S(2)}, u32[]{:S(2)}) %collective-permute-start.10) | collective-permute-done | bytes 4128 | tf_op jit(solution)/shard_map/ppermute | solution.py:246
  34.3 1.8 %collective-permute-done.9.above_ref = f32[8,128]{1,0:T(8,128)S(1)} collective-permute-done((f32[8,128]{1,0:T(8,128)S(1)}, f32[8,128]{1,0:T(8,128)S(1)}, u32[]{:S(2)}, u32[]{:S(2)}) %collective-permute-start.9) | collective-permute-done | bytes 4128 | tf_op jit(solution)/shard_map/ppermute | solution.py:246
  36.1 0.8 %relax.1 = (f32[1,2,4,8]{3,2,1,0:T(4,128)}, f32[1,2,4,8]{3,2,1,0:T(4,128)}) custom-call(f32[8,128]{1,0:T(8,128)S(1)} %window.1.own_ref, f32[8,128]{1,0:T(8,128)S(1)} %collective-permute-done.9.above_ref, f32[8,128]{1,0:T(8,128)S(1)} %collective-permute-done.10.below_ref), custom_call_target="tpu_custom_call" | custom-call | tf_op jit(solution)/shard_map/relax/pallas_call | solution.py:151
  (1 shorter events, 0.0 us)
Async XLA Ops:
  0.6 1.0 %copy-start = (f32[1,256,512]{2,1,0:T(8,128)S(1)}, f32[1,256,512]{2,1,0:T(8,128)}, u32[]{:S(2)}) copy-start(f32[1,256,512]{2,1,0:T(8,128)} %param.4) | copy-start | bytes 1572868
  1.8 17.8 %collective-permute-start.3 = (f32[256,288]{1,0:T(8,128)S(1)}, f32[256,288]{1,0:T(8,128)S(1)}, u32[]{:S(2)}, u32[]{:S(2)}) collective-permute-start(f32[256,288]{1,0:T(8,128)S(1)} %cut.1), channel_id=1, source_target_pairs={{0,16},{16,0},{17,1},{1,17},{2,18},{18,2},{19,3},{3,19},{4,20},{20... | collective-permute-start | bytes 884744 | tf_op jit(solution)/shard_map/ppermute | solution.py:241
  4.8 3.7 %collective-permute-start = (f32[32,512]{1,0:T(8,128)S(1)}, f32[32,512]{1,0:T(8,128)S(1)}, u32[]{:S(2)}, u32[]{:S(2)}) collective-permute-start(f32[32,512]{1,0:T(8,128)S(1)} %get-tuple-element.7), channel_id=1, source_target_pairs={{0,4},{4,8},{8,12},{12,0},{1,5},{5,9},{9,13},{13,1},{2,6},{6,10},{... | collective-permute-start | bytes 196616 | tf_op jit(solution)/shard_map/ppermute | solution.py:246
  4.8 14.8 %copy-start.1 = (bf16[2,256,256]{2,1,0:T(8,128)(2,1)S(1)}, bf16[2,256,256]{2,1,0:T(8,128)(2,1)}, u32[]{:S(2)}) copy-start(bf16[2,256,256]{2,1,0:T(8,128)(2,1)} %constant.7.clone.right_ref) | copy-start | bytes 786436
  4.9 14.8 %copy-start.2 = (bf16[128,432]{1,0:T(8,128)(2,1)S(1)}, bf16[128,432]{1,0:T(8,128)(2,1)}, u32[]{:S(2)}) copy-start(bf16[128,432]{1,0:T(8,128)(2,1)} %constant.8.clone.back_ref) | copy-start | bytes 331780
  4.9 14.8 %copy-start.3 = (bf16[144,384]{1,0:T(8,128)(2,1)S(1)}, bf16[144,384]{1,0:T(8,128)(2,1)}, u32[]{:S(2)}) copy-start(bf16[144,384]{1,0:T(8,128)(2,1)} %constant.6.clone.left_ref) | copy-start | bytes 331780
  4.9 3.6 %collective-permute-start.1 = (f32[32,512]{1,0:T(8,128)S(1)}, f32[32,512]{1,0:T(8,128)S(1)}, u32[]{:S(2)}, u32[]{:S(2)}) collective-permute-start(f32[32,512]{1,0:T(8,128)S(1)} %get-tuple-element.8), channel_id=1, source_target_pairs={{0,12},{4,0},{8,4},{12,8},{1,13},{5,1},{9,5},{13,9},{2,14},{6,2},{... | collective-permute-start | bytes 196616 | tf_op jit(solution)/shard_map/ppermute | solution.py:246
  8.7 10.9 %collective-permute-start.4 = (f32[64,288]{1,0:T(8,128)S(1)}, f32[64,288]{1,0:T(8,128)S(1)}, u32[]{:S(2)}, u32[]{:S(2)}) collective-permute-start(f32[64,288]{1,0:T(8,128)S(1)} %get-tuple-element.10), channel_id=1, source_target_pairs={{0,16},{16,0},{17,1},{1,17},{2,18},{18,2},{19,3},{3,19},{4,20},{20... | collective-permute-start | bytes 221192 | tf_op jit(solution)/shard_map/ppermute | solution.py:241
  9.1 5.8 %collective-permute-start.2 = (f32[80,128]{1,0:T(8,128)S(1)}, f32[80,128]{1,0:T(8,128)S(1)}, u32[]{:S(2)}, u32[]{:S(2)}) collective-permute-start(f32[80,128]{1,0:T(8,128)S(1)} %get-tuple-element.9), channel_id=1, source_target_pairs={{0,3},{16,17},{17,16},{1,2},{2,1},{18,19},{19,18},{3,0},{4,7},{20,... | collective-permute-start | bytes 122888 | tf_op jit(solution)/shard_map/ppermute | solution.py:241
  12.9 6.8 %collective-permute-start.5 = (f32[80,128]{1,0:T(8,128)S(1)}, f32[80,128]{1,0:T(8,128)S(1)}, u32[]{:S(2)}, u32[]{:S(2)}) collective-permute-start(f32[80,128]{1,0:T(8,128)S(1)} %get-tuple-element.11), channel_id=1, source_target_pairs={{0,17},{16,3},{17,2},{1,16},{2,19},{18,1},{19,0},{3,18},{4,21},{20... | collective-permute-start | bytes 122888 | tf_op jit(solution)/shard_map/ppermute | solution.py:241
  25.4 4.5 %collective-permute-start.8 = (f32[8,128]{1,0:T(8,128)S(1)}, f32[8,128]{1,0:T(8,128)S(1)}, u32[]{:S(2)}, u32[]{:S(2)}) collective-permute-start(f32[8,128]{1,0:T(8,128)S(1)} %flow.1.own_ref), channel_id=1, source_target_pairs={{0,19},{16,1},{17,0},{1,18},{2,17},{18,3},{19,2},{3,16},{4,23},{20... | collective-permute-start | bytes 12296 | tf_op jit(solution)/shard_map/ppermute | solution.py:241
  27.5 5.4 %collective-permute-start.7 = (f32[8,128]{1,0:T(8,128)S(1)}, f32[8,128]{1,0:T(8,128)S(1)}, u32[]{:S(2)}, u32[]{:S(2)}) collective-permute-start(f32[8,128]{1,0:T(8,128)S(1)} %flow.1.own_ref), channel_id=1, source_target_pairs={{0,3},{16,17},{17,16},{1,2},{2,1},{18,19},{19,18},{3,0},{4,7},{20,... | collective-permute-start | bytes 12296 | tf_op jit(solution)/shard_map/ppermute | solution.py:241
  27.6 5.3 %collective-permute-start.6 = (f32[8,128]{1,0:T(8,128)S(1)}, f32[8,128]{1,0:T(8,128)S(1)}, u32[]{:S(2)}, u32[]{:S(2)}) collective-permute-start(f32[8,128]{1,0:T(8,128)S(1)} %flow.1.own_ref), channel_id=1, source_target_pairs={{0,16},{16,0},{17,1},{1,17},{2,18},{18,2},{19,3},{3,19},{4,20},{20... | collective-permute-start | bytes 12296 | tf_op jit(solution)/shard_map/ppermute | solution.py:241
  33.0 1.3 %collective-permute-start.10 = (f32[8,128]{1,0:T(8,128)S(1)}, f32[8,128]{1,0:T(8,128)S(1)}, u32[]{:S(2)}, u32[]{:S(2)}) collective-permute-start(f32[8,128]{1,0:T(8,128)S(1)} %window.1.own_ref), channel_id=1, source_target_pairs={{0,12},{4,0},{8,4},{12,8},{1,13},{5,1},{9,5},{13,9},{2,14},{6,2},{... | collective-permute-start | bytes 12296 | tf_op jit(solution)/shard_map/ppermute | solution.py:246
  33.0 3.1 %collective-permute-start.9 = (f32[8,128]{1,0:T(8,128)S(1)}, f32[8,128]{1,0:T(8,128)S(1)}, u32[]{:S(2)}, u32[]{:S(2)}) collective-permute-start(f32[8,128]{1,0:T(8,128)S(1)} %window.1.own_ref), channel_id=1, source_target_pairs={{0,4},{4,8},{8,12},{12,0},{1,5},{5,9},{9,13},{13,1},{2,6},{6,10},{... | collective-permute-start | bytes 12296 | tf_op jit(solution)/shard_map/ppermute | solution.py:246

commit v4 on v3

--- a/solution.py
+++ b/solution.py
@@ -68,10 +68,14 @@
                 high_ref, low_ref, *scratch):
     for z in range(2):
         keep_region(region_ref[z], z, cols * STRIDE, high_ref, low_ref)
-    correlate(rows, cols, group, left_ref, right_ref, back_ref, flow_ref, high_ref, low_ref, *scratch)
-
-
-def correlate(rows, cols, group, left_ref, right_ref, back_ref, flow_ref,
+
+    def put(c, i, row):
+        flow_ref[c * rows + i:c * rows + i + 1, :] = row
+
+    correlate(rows, cols, group, left_ref, right_ref, back_ref, put, high_ref, low_ref, *scratch)
+
+
+def correlate(rows, cols, group, left_ref, right_ref, back_ref, put,
               high_ref, low_ref, half_ref, peak_ref, mass_ref, tilt_ref):
     order = [2 * t for t in range(cols // 2)] + [2 * t + 1 for t in range(cols // 2)]
     for z in range(2):
@@ -125,9 +129,7 @@
     for c, value in enumerate((flow_y, flow_x)):
         spread = jnp.where(here, value, 0.0)
         for i in range(rows):
-            flow_ref[c * rows + i:c * rows + i + 1, :] = jnp.sum(
-                spread[i * cols:(i + 1) * cols], axis=0, keepdims=True
-            )
+            put(c, i, jnp.sum(spread[i * cols:(i + 1) * cols], axis=0, keepdims=True))
 
 
 def flow_scratch(rows, cols):
@@ -241,11 +243,6 @@
     return lax.ppermute(value, AXES, pairs)
 
 
-def ring(value, axis, by):
-    size = lax.axis_size(axis)
-    return lax.ppermute(value, axis, [(i, (i + by) % size) for i in range(size)])
-
-
 def mate(g):
     return g ^ 1
 
@@ -254,12 +251,25 @@
     return g - 1 if g % 2 == 0 else g + 1
 
 
-def far(g):
-    return g - 2 if g % 2 == 0 else g + 2
-
-
 def past(g):
     return g + 2 if g % 2 == 0 else g - 2
+
+
+def pairs_even(value):
+    size = lax.axis_size("ty")
+    return lax.ppermute(value, "ty", [(i, i ^ 1) for i in range(size)])
+
+
+def pairs_odd(value):
+    size = lax.axis_size("ty")
+    return lax.ppermute(value, "ty", [(i, (i - 1 if i % 2 == 0 else i + 1) % size) for i in range(size)])
+
+
+def around(y, ny, even, odd):
+    lower = y % 2 == 1
+    above = jnp.where(y == 0, 0.0, jnp.where(lower, even, odd))
+    below = jnp.where(y == ny - 1, 0.0, jnp.where(lower, odd, even))
+    return above, below
 
 
 def where_am_i():
@@ -267,22 +277,32 @@
     return section, y, x, (section + x) % 2
 
 
-def cut_kernel(core, tile_ref, out_ref):
-    _, _, _, half = where_am_i()
-    width = tile_ref.shape[1]
+def stack_rows(parts, start, stop):
+    taken, base = [], 0
+    for height, rows in parts:
+        low, high = max(start - base, 0), min(stop - base, height)
+        if low < high:
+            taken.append(rows(low, high))
+        base += height
+    return taken[0] if len(taken) == 1 else jnp.concatenate(taken, axis=0)
+
+
+def cut_kernel(core, upper, tile_ref, out_ref, even_ref, odd_ref):
+    _, y, _, half = where_am_i()
+    tall, width = tile_ref.shape
 
     @pl.when(half == 0)
     def _():
-        out_ref[...] = tile_ref[:, width - core:]
+        out_ref[...] = tile_ref[:upper, width - core:]
 
     @pl.when(half == 1)
     def _():
-        out_ref[...] = tile_ref[:, :core]
-
-
-def strips_kernel(tile_ref, first_ref, last_ref):
-    first_ref[...] = tile_ref[:HALF]
-    last_ref[...] = tile_ref[tile_ref.shape[0] - HALF:]
+        out_ref[...] = tile_ref[:upper, :core]
+
+    first, last = tile_ref[:HALF], tile_ref[tall - HALF:]
+    lower = y % 2 == 1
+    even_ref[...] = jnp.where(lower, first, last)
+    odd_ref[...] = jnp.where(lower, last, first)
 
 
 def packed(column):
@@ -294,11 +314,10 @@
     return jnp.concatenate([block[:, q * HALF:(q + 1) * HALF] for q in range(4)], axis=0)
 
 
-def borders_kernel(core, ny, tile_ref, above_ref, below_ref, strips_ref, near_ref, past_ref):
+def borders_kernel(core, upper, ny, tile_ref, even_ref, odd_ref, above_ref, rest_ref, near_ref, past_ref):
     _, y, _, half = where_am_i()
     width = tile_ref.shape[1]
-    above = jnp.where(y == 0, 0.0, above_ref[...])
-    below = jnp.where(y == ny - 1, 0.0, below_ref[...])
+    above, below = around(y, ny, even_ref[...], odd_ref[...])
 
     def column(lanes):
         return packed(jnp.concatenate([above[:, lanes], tile_ref[:, lanes], below[:, lanes]], axis=0))
@@ -306,64 +325,92 @@
     start, end = slice(0, HALF), slice(width - HALF, width)
     first, last = column(start), column(end)
 
+    def send(lanes):
+        above_ref[...] = above[:, lanes]
+        rest_ref[...] = jnp.concatenate([tile_ref[upper:, lanes], below[:, lanes]], axis=0)
+
     @pl.when(half == 0)
     def _():
-        strips_ref[:HALF], strips_ref[HALF:] = above[:, width - core:], below[:, width - core:]
+        send(slice(width - core, width))
         near_ref[...], past_ref[...] = first, last
 
     @pl.when(half == 1)
     def _():
-        strips_ref[:HALF], strips_ref[HALF:] = above[:, :core], below[:, :core]
+        send(slice(0, core))
         near_ref[...], past_ref[...] = last, first
 
 
-def shared_kernel(rows, cols, group, ny, nx, tile_ref, above_ref, below_ref, side_ref,
-                  other_ref, strips_ref, other_side_ref, left_ref, right_ref, back_ref, flow_ref,
+def shared_kernel(first_row, rows, all_rows, cols, group, ny, nx, tile_ref, even_ref, odd_ref, side_ref,
+                  other_refs, other_side_ref, before_ref, left_ref, right_ref, back_ref, flow_ref,
                   high_ref, low_ref, *scratch):
     section, y, x, half = where_am_i()
-    core, width = other_ref.shape[1], tile_ref.shape[1]
+    core, (tall, width) = other_refs[0].shape[1], tile_ref.shape
     wide = cols * STRIDE
+    start, stop = first_row * STRIDE, (first_row + rows + 1) * STRIDE
     at_end = jnp.where(half == 0, x == 0, x == nx - 1)
-    own_side = jnp.where(at_end, 0.0, unpacked(side_ref[...]))
-    other_side = jnp.where(at_end, 0.0, unpacked(other_side_ref[...]))
-    above = jnp.where(y == 0, 0.0, above_ref[...])
-    below = jnp.where(y == ny - 1, 0.0, below_ref[...])
-    other = jnp.concatenate([strips_ref[:HALF], other_ref[...], strips_ref[HALF:]], axis=0)
+    own_side = jnp.where(at_end, 0.0, unpacked(side_ref[...])[start:stop])
+    other_side = jnp.where(at_end, 0.0, unpacked(other_side_ref[...])[start:stop])
+    above, below = around(y, ny, even_ref[...], odd_ref[...])
+    parts = [(ref.shape[0], lambda low, high, ref=ref: ref[low:high]) for ref in other_refs]
+    other = stack_rows(parts, start, stop)
+
+    def own(lanes):
+        parts = [(HALF, lambda low, high: above[low:high, lanes]),
+                 (tall, lambda low, high: tile_ref[low:high, lanes]),
+                 (HALF, lambda low, high: below[low:high, lanes])]
+        return stack_rows(parts, start, stop)
 
     @pl.when(half == 0)
     def _():
-        own = jnp.concatenate([above[:, :core], tile_ref[:, :core], below[:, :core]], axis=0)
-        keep_region(jnp.concatenate([own_side, own], axis=1), section, wide, high_ref, low_ref)
+        value = jnp.concatenate([own_side, own(slice(0, core))], axis=1)
+        keep_region(value, section, wide, high_ref, low_ref)
         keep_region(jnp.concatenate([other_side, other], axis=1), 1 - section, wide, high_ref, low_ref)
 
     @pl.when(half == 1)
     def _():
-        lanes = slice(width - core, width)
-        own = jnp.concatenate([above[:, lanes], tile_ref[:, lanes], below[:, lanes]], axis=0)
-        keep_region(jnp.concatenate([own, own_side], axis=1), section, wide, high_ref, low_ref)
+        value = jnp.concatenate([own(slice(width - core, width)), own_side], axis=1)
+        keep_region(value, section, wide, high_ref, low_ref)
         keep_region(jnp.concatenate([other, other_side], axis=1), 1 - section, wide, high_ref, low_ref)
 
-    correlate(rows, cols, group, left_ref, right_ref, back_ref, flow_ref, high_ref, low_ref, *scratch)
-
-
-def window_kernel(width, nx, own_ref, mate_ref, near_ref, far_ref, out_ref):
-    _, _, x, place = where_am_i()
-    half = place == 1
-    own, other, close, beyond = own_ref[...], mate_ref[...], near_ref[...], far_ref[...]
-    lane = lax.broadcasted_iota(jnp.int32, own.shape, 1)
-    begin = jnp.where(x == 0, 0.0, jnp.where(half, beyond, close))
-    left = jnp.where(half, other, own)
-    right = jnp.where(half, own, other)
-    end = jnp.where(x == nx - 1, 0.0, jnp.where(half, close, beyond))
-    begin, left = pltpu.roll(begin, PATCH + 2 - width, 1), pltpu.roll(left, 2, 1)
-    right, end = pltpu.roll(right, 2 + width, 1), pltpu.roll(end, 2 + 2 * width, 1)
-    value = jnp.where(lane < 2, begin, jnp.where(lane < 2 + width, left, right))
-    value = jnp.where(lane < 2 + 2 * width, value, jnp.where(lane < 4 + 2 * width, end, 0.0))
-    out_ref[...] = value
-
-
-def relax_kernel(rows, cols, ny, nx, own_ref, above_ref, below_ref, mesh_ref, earlier_ref):
+    flow_ref[...] = jnp.zeros_like(flow_ref) if before_ref is None else before_ref[...]
+
+    def put(c, i, row):
+        at = c * all_rows + first_row + i
+        flow_ref[at:at + 1, :] = row
+
+    correlate(rows, cols, group, left_ref, right_ref, back_ref, put, high_ref, low_ref, *scratch)
+
+
+def upper_kernel(dims, tile, even, odd, side, above, other, other_side, left, right, back, *rest):
+    shared_kernel(0, *dims, tile, even, odd, side, [above, other], other_side, None, left, right, back, *rest)
+
+
+def lower_kernel(first_row, dims, tile, even, odd, side, above, other, more, other_side, before,
+                 left, right, back, *rest):
+    shared_kernel(first_row, *dims, tile, even, odd, side, [above, other, more], other_side, before,
+                  left, right, back, *rest)
+
+
+def close_kernel(width, nx, own_ref, near_ref, out_ref):
+    _, _, x, half = where_am_i()
+    own, lane = own_ref[...], lax.broadcasted_iota(jnp.int32, own_ref.shape, 1)
+    close = jnp.where(jnp.where(half == 0, x == 0, x == nx - 1), 0.0, near_ref[...])
+    begin = jnp.where(lane < 2, pltpu.roll(close, PATCH + 2 - width, 1), pltpu.roll(own, 2, 1))
+    end = jnp.where(lane < width, own, pltpu.roll(close, width, 1))
+    out_ref[...] = jnp.where(lane < width + 2, jnp.where(half == 0, begin, end), 0.0)
+
+
+def window_kernel(width, own_ref, mate_ref, out_ref):
+    _, _, _, half = where_am_i()
+    own, other = own_ref[...], mate_ref[...]
+    left, right = jnp.where(half == 0, own, other), jnp.where(half == 0, other, own)
+    out_ref[...] = left + pltpu.roll(right, width + 2, 1)
+
+
+def relax_kernel(rows, cols, ny, nx, own_ref, even_ref, odd_ref, mesh_ref, earlier_ref):
     section, y, x, _ = where_am_i()
+    above, below = around(y, ny, even_ref[...], odd_ref[...])
+    own = own_ref[...]
     tall = rows + 4
     shape = (tall, PATCH)
     row = lax.broadcasted_iota(jnp.int32, shape, 0) - 2 + y * rows
@@ -371,17 +418,17 @@
     inside = (row >= 0) & (row < ny * rows) & (col >= 0) & (col < nx * cols)
 
     def step(mesh, flow):
-        around = (
+        nearby = (
             pltpu.roll(mesh, 1, 0) + pltpu.roll(mesh, tall - 1, 0)
             + pltpu.roll(mesh, 1, 1) + pltpu.roll(mesh, PATCH - 1, 1)
         )
-        lap = around - 4.0 * mesh
+        lap = nearby - 4.0 * mesh
         return jnp.where(inside, mesh + rate * (stiffness * lap + flow - mesh), 0.0)
 
     for c in range(2):
         flow = jnp.concatenate(
-            [above_ref[(c + 1) * rows - 2:(c + 1) * rows], own_ref[c * rows:(c + 1) * rows],
-             below_ref[c * rows:c * rows + 2]], axis=0)
+            [above[(c + 1) * rows - 2:(c + 1) * rows], own[c * rows:(c + 1) * rows],
+             below[c * rows:c * rows + 2]], axis=0)
         flow = jnp.where(inside, flow, 0.0)
         mesh = step(step(flow, flow), flow)
         mesh = pltpu.roll(pltpu.roll(mesh, tall - 2, 0), PATCH - 2, 1)[:rows, :cols]
@@ -393,41 +440,53 @@
     tile = images[0]
     ny, nx = lax.axis_size("ty"), lax.axis_size("tx")
     rows, cols = tile.shape[0] // STRIDE, tile.shape[1] // STRIDE
-    half = cols // 2
-    core = half * STRIDE + HALF
+    half, early = cols // 2, rows // 2
+    core, upper = half * STRIDE + HALF, early * STRIDE + HALF
     tall = tile.shape[0] + 2 * HALF
 
-    payload = kernel_call(functools.partial(cut_kernel, core), floats(tile.shape[0], core), tile, name="cut")
+    strip = floats(HALF, tile.shape[1])
+    payload, even, odd = kernel_call(
+        functools.partial(cut_kernel, core, upper), (floats(upper, core), strip, strip), tile, name="cut",
+    )
     other = along(payload, mate)
-    strip = floats(HALF, tile.shape[1])
-    first, last = kernel_call(strips_kernel, (strip, strip), tile, name="strips")
-    above, below = ring(last, "ty", 1), ring(first, "ty", -1)
+    even, odd = pairs_even(even), pairs_odd(odd)
     edge = floats(tall // 4, 4 * HALF)
-    strips, edge_near, edge_past = kernel_call(
-        functools.partial(borders_kernel, core, ny), (floats(2 * HALF, core), edge, edge),
-        tile, above, below, name="borders",
-    )
-    strips, side, other_side = along(strips, mate), along(edge_near, near), along(edge_past, past)
+    above, rest, edge_near, edge_past = kernel_call(
+        functools.partial(borders_kernel, core, upper, ny),
+        (floats(HALF, core), floats(tile.shape[0] - upper + HALF, core), edge, edge),
+        tile, even, odd, name="borders",
+    )
+    above, side, other_side = along(above, mate), along(edge_near, near), along(edge_past, past)
+    more = along(rest, mate)
+    constants = tables()
     flow = kernel_call(
-        functools.partial(shared_kernel, rows, half, 4, ny, nx), floats(2 * rows, PATCH),
-        tile, above, below, side, other, strips, other_side, *tables(),
-        scratch=flow_scratch(rows, half), name="flow",
+        functools.partial(upper_kernel, (early, rows, half, 4, ny, nx)), floats(2 * rows, PATCH),
+        tile, even, odd, side, above, other, other_side, *constants,
+        scratch=flow_scratch(early, half), name="upper",
+    )
+    flow = kernel_call(
+        functools.partial(lower_kernel, early, (rows - early, rows, half, 4, ny, nx)), floats(2 * rows, PATCH),
+        tile, even, odd, side, above, other, more, other_side, flow, *constants,
+        scratch=flow_scratch(rows - early, half), name="lower",
+    )
+    close = kernel_call(
+        functools.partial(close_kernel, half, nx), floats(*flow.shape), flow, along(flow, near), name="close",
     )
     window = kernel_call(
-        functools.partial(window_kernel, half, nx), floats(*flow.shape),
-        flow, along(flow, mate), along(flow, near), along(flow, far), name="window",
+        functools.partial(window_kernel, half), floats(*flow.shape), close, along(close, mate), name="window",
     )
     out = floats(1, 2, rows, cols)
     return kernel_call(
         functools.partial(relax_kernel, rows, cols, ny, nx), (out, out),
-        window, ring(window, "ty", 1), ring(window, "ty", -1), name="relax", last=True,
+        window, pairs_even(window), pairs_odd(window), name="relax", last=True,
     )
 
 
 def solution(mesh):
     in_specs = (P("sec", "ty", "tx"),)
     out_specs = (P("sec", None, "ty", "tx"), P("sec", None, "ty", "tx"))
-    shared = mesh.shape["sec"] == 2
+    even = mesh.shape["ty"] % 2 == 0 and mesh.shape["tx"] % 2 == 0
+    shared = mesh.shape["sec"] == 2 and even
     return jax.shard_map(
         shared_section if shared else whole_sections,
         mesh=mesh, in_specs=in_specs, out_specs=out_specs, check_vma=False,

time: 37.1 us -> 39 us (1.051)
  starting transfers between devices: 12.9 us -> 16 us
  waiting for transfers between devices: 15.3 us -> 13.4 us
  Pallas kernels: 6.95 us -> 7.72 us
    ppermute x4, starting transfers between devices: 2.27 us -> 4.75 us  [the longest x2 2.59 us: pairs_odd(): lax.ppermute(value, 'ty', [(i, (i - 1 if i % 2 == 0 else i + 1) % size) f...]
    ppermute x4, waiting for transfers between devices: 4.55 us -> 2.4 us  [the longest x2 2.4 us: pairs_odd(): lax.ppermute(value, 'ty', [(i, (i - 1 if i % 2 == 0 else i + 1) % size) f...]
    pallas_call x6 -> x7, Pallas kernels: 6.95 us -> 7.72 us  [kernel_call(): pl.pallas_call(body, out_shape=shapes, in_specs=[IN_VMEM] * len(args), ou...]
    ppermute x7, starting transfers between devices: 10.6 us -> 11.2 us  [along(): return lax.ppermute(value, AXES, pairs)]
  transfers between devices with their start and end apart: 11 -> 11, of which waited for: 7 -> 6; matrix products, arithmetic and copies ran while one was open for 0% -> 0% of each run, Pallas kernels for 1% -> 9%
where the time goes in v4:
time: 39 us; the launch traced here: 38.8 us
  starting transfers between devices  16 us (41%)
  waiting for transfers between devices  13.4 us (34%)
  Pallas kernels  7.72 us (20%)
  local copies, waits for them, and re-layouts  1.05 us (3%)
  between operations  0.69 us (2%)
    ppermute x7, starting transfers between devices, along(): return lax.ppermute(value, AXES, pairs)  11.2 us
    ppermute x7, waiting for transfers between devices, along(): return lax.ppermute(value, AXES, pairs)  11 us
    pallas_call x7, Pallas kernels, kernel_call(): pl.pallas_call(body, out_shape=shapes, in_specs=[IN_VMEM] * len(args), ou...  7.72 us
    ppermute x2, starting transfers between devices, pairs_odd(): lax.ppermute(value, 'ty', [(i, (i - 1 if i % 2 == 0 else i + 1) % size) f...  2.59 us
    ppermute x2, waiting for transfers between devices, pairs_odd(): lax.ppermute(value, 'ty', [(i, (i - 1 if i % 2 == 0 else i + 1) % size) f...  2.4 us
    ppermute x2, starting transfers between devices, pairs_even(): return lax.ppermute(value, 'ty', [(i, i ^ 1) for i in range(size)])  2.16 us
    unnamed x8, local copies, waits for them, and re-layouts  1.05 us
  transfers between devices with their start and end apart: 11, of which 6 were waited for; matrix products, arithmetic and copies ran while one was open for 0% of the time, Pallas kernels for 9%

profile of v4, /device:TPU:0, one launch (start us, length us, event | category | flops | bytes accessed | tf_op | source)
XLA Modules:
  0.0 38.8 jit_solution(4908608558803666093)
XLA Ops:
  0.6 0.0 copy-start
  0.6 1.0 %copy-done = f32[1,256,512]{2,1,0:T(8,128)S(1)} copy-done((f32[1,256,512]{2,1,0:T(8,128)S(1)}, f32[1,256,512]{2,1,0:T(8,128)}, u32[]{:S(2)}) %copy-start) | copy-done | bytes 524312
  1.7 0.1 cut.1
  1.8 0.6 %collective-permute-start = (f32[32,512]{1,0:T(8,128)S(1)}, f32[32,512]{1,0:T(8,128)S(1)}, u32[]{:S(2)}, u32[]{:S(2)}) collective-permute-start(f32[32,512]{1,0:T(8,128)S(1)} %get-tuple-element.9), channel_id=1, source_target_pairs={{0,4},{4,0},{8,12},{12,8},{1,5},{5,1},{9,13},{13,9},{2,6},{6,2},{1... | collective-permute-start | bytes 196616 | tf_op jit(solution)/shard_map/ppermute | solution.py:260
  2.4 2.6 %collective-permute-start.1 = (f32[32,512]{1,0:T(8,128)S(1)}, f32[32,512]{1,0:T(8,128)S(1)}, u32[]{:S(2)}, u32[]{:S(2)}) collective-permute-start(f32[32,512]{1,0:T(8,128)S(1)} %get-tuple-element.10), channel_id=1, source_target_pairs={{0,12},{4,8},{8,4},{12,0},{1,13},{5,9},{9,5},{13,1},{2,14},{6,10},... | collective-permute-start | bytes 196616 | tf_op jit(solution)/shard_map/ppermute | solution.py:265
  5.0 0.0 copy-start.1
  5.0 0.0 copy-start.2
  5.0 0.0 copy-start.3
  5.0 1.4 %collective-permute-start.4 = (f32[160,288]{1,0:T(8,128)S(1)}, f32[160,288]{1,0:T(8,128)S(1)}, u32[]{:S(2)}, u32[]{:S(2)}) collective-permute-start(f32[160,288]{1,0:T(8,128)S(1)} %get-tuple-element.13), channel_id=1, source_target_pairs={{0,16},{16,0},{17,1},{1,17},{2,18},{18,2},{19,3},{3,19},{4,20},{20... | collective-permute-start | bytes 552968 | tf_op jit(solution)/shard_map/ppermute | solution.py:243
  6.4 0.0 collective-permute-done.even_ref.even
  6.4 1.0 %collective-permute-done.1.odd_ref.odd = f32[32,512]{1,0:T(8,128)S(1)} collective-permute-done((f32[32,512]{1,0:T(8,128)S(1)}, f32[32,512]{1,0:T(8,128)S(1)}, u32[]{:S(2)}, u32[]{:S(2)}) %collective-permute-start.1) | collective-permute-done | bytes 65568 | tf_op jit(solution)/shard_map/ppermute | solution.py:265
  7.4 0.2 borders.1
  7.6 1.2 %collective-permute-start.5 = (f32[128,288]{1,0:T(8,128)S(1)}, f32[128,288]{1,0:T(8,128)S(1)}, u32[]{:S(2)}, u32[]{:S(2)}) collective-permute-start(f32[128,288]{1,0:T(8,128)S(1)} %get-tuple-element.14), channel_id=1, source_target_pairs={{0,16},{16,0},{17,1},{1,17},{2,18},{18,2},{19,3},{3,19},{4,20},{20... | collective-permute-start | bytes 442376 | tf_op jit(solution)/shard_map/ppermute | solution.py:243
  8.9 3.8 %collective-permute-start.2 = (f32[80,128]{1,0:T(8,128)S(1)}, f32[80,128]{1,0:T(8,128)S(1)}, u32[]{:S(2)}, u32[]{:S(2)}) collective-permute-start(f32[80,128]{1,0:T(8,128)S(1)} %get-tuple-element.11), channel_id=1, source_target_pairs={{0,3},{16,17},{17,16},{1,2},{2,1},{18,19},{19,18},{3,0},{4,7},{20,... | collective-permute-start | bytes 122888 | tf_op jit(solution)/shard_map/ppermute | solution.py:243
  12.7 0.0 collective-permute-start.6
  12.7 1.5 %collective-permute-start.3 = (f32[32,288]{1,0:T(8,128)S(1)}, f32[32,288]{1,0:T(8,128)S(1)}, u32[]{:S(2)}, u32[]{:S(2)}) collective-permute-start(f32[32,288]{1,0:T(8,128)S(1)} %get-tuple-element.12), channel_id=1, source_target_pairs={{0,16},{16,0},{17,1},{1,17},{2,18},{18,2},{19,3},{3,19},{4,20},{20... | collective-permute-start | bytes 110600 | tf_op jit(solution)/shard_map/ppermute | solution.py:243
  14.1 4.5 %collective-permute-done.3.above = f32[32,288]{1,0:T(8,128)S(1)} collective-permute-done((f32[32,288]{1,0:T(8,128)S(1)}, f32[32,288]{1,0:T(8,128)S(1)}, u32[]{:S(2)}, u32[]{:S(2)}) %collective-permute-start.3) | collective-permute-done | bytes 36896 | tf_op jit(solution)/shard_map/ppermute | solution.py:243
  18.6 0.0 collective-permute-done.2.side
  18.6 0.7 %collective-permute-done.6.other_side = f32[80,128]{1,0:T(8,128)S(1)} collective-permute-done((f32[80,128]{1,0:T(8,128)S(1)}, f32[80,128]{1,0:T(8,128)S(1)}, u32[]{:S(2)}, u32[]{:S(2)}) %collective-permute-start.6) | collective-permute-done | bytes 40992 | tf_op jit(solution)/shard_map/ppermute | solution.py:243
  19.4 0.0 collective-permute-done.4.other
  19.4 0.0 copy-done.1
  19.4 0.0 copy-done.2
  19.4 0.0 copy-done.3
  19.4 3.2 %upper.1.before = f32[8,128]{1,0:T(8,128)S(1)} custom-call(f32[256,512]{1,0:T(8,128)S(1)} %bitcast.3, f32[32,512]{1,0:T(8,128)S(1)} %collective-permute-done.even_ref.even, f32[32,512]{1,0:T(8,128)S(1)} %collective-permute-done.1.odd_ref.odd, f32[80,128]{1,0:T(8,128)S(1)} %collective-permute-done.2.side, f32[32,288]{1,0:T(8,128)S(1)} %collective-permute-done.3.above, ...), custom_call_target="tpu_custom_call" | custom-call | tf_op jit(solution)/shard_map/upper/pallas_call | solution.py:153
  22.6 0.0 collective-permute-done.5.more
  22.6 3.2 %lower.1.own_ref = f32[8,128]{1,0:T(8,128)S(1)} custom-call(f32[256,512]{1,0:T(8,128)S(1)} %bitcast.4, f32[32,512]{1,0:T(8,128)S(1)} %collective-permute-done.even_ref.even, f32[32,512]{1,0:T(8,128)S(1)} %collective-permute-done.1.odd_ref.odd, f32[80,128]{1,0:T(8,128)S(1)} %collective-permute-done.2.side, f32[32,288]{1,0:T(8,128)S(1)} %collective-permute-done.3.above, ...), custom_call_target="tpu_custom_call" | custom-call | tf_op jit(solution)/shard_map/lower/pallas_call | solution.py:153
  25.8 3.3 %collective-permute-start.7 = (f32[8,128]{1,0:T(8,128)S(1)}, f32[8,128]{1,0:T(8,128)S(1)}, u32[]{:S(2)}, u32[]{:S(2)}) collective-permute-start(f32[8,128]{1,0:T(8,128)S(1)} %lower.1.own_ref), channel_id=1, source_target_pairs={{0,3},{16,17},{17,16},{1,2},{2,1},{18,19},{19,18},{3,0},{4,7},{20,... | collective-permute-start | bytes 12296 | tf_op jit(solution)/shard_map/ppermute | solution.py:243
  29.0 2.2 %collective-permute-done.7.near_ref = f32[8,128]{1,0:T(8,128)S(1)} collective-permute-done((f32[8,128]{1,0:T(8,128)S(1)}, f32[8,128]{1,0:T(8,128)S(1)}, u32[]{:S(2)}, u32[]{:S(2)}) %collective-permute-start.7) | collective-permute-done | bytes 4128 | tf_op jit(solution)/shard_map/ppermute | solution.py:243
  31.2 0.1 close.1.own_ref
  31.3 0.0 collective-permute-start.8
  31.3 3.6 %collective-permute-done.8.mate_ref = f32[8,128]{1,0:T(8,128)S(1)} collective-permute-done((f32[8,128]{1,0:T(8,128)S(1)}, f32[8,128]{1,0:T(8,128)S(1)}, u32[]{:S(2)}, u32[]{:S(2)}) %collective-permute-start.8) | collective-permute-done | bytes 4128 | tf_op jit(solution)/shard_map/ppermute | solution.py:243
  34.9 0.1 window.1.own_ref
  35.0 0.0 collective-permute-start.10
  35.0 1.6 %collective-permute-start.9 = (f32[8,128]{1,0:T(8,128)S(1)}, f32[8,128]{1,0:T(8,128)S(1)}, u32[]{:S(2)}, u32[]{:S(2)}) collective-permute-start(f32[8,128]{1,0:T(8,128)S(1)} %window.1.own_ref), channel_id=1, source_target_pairs={{0,4},{4,0},{8,12},{12,8},{1,5},{5,1},{9,13},{13,9},{2,6},{6,2},{1... | collective-permute-start | bytes 12296 | tf_op jit(solution)/shard_map/ppermute | solution.py:260
  36.6 1.4 %collective-permute-done.10.odd_ref = f32[8,128]{1,0:T(8,128)S(1)} collective-permute-done((f32[8,128]{1,0:T(8,128)S(1)}, f32[8,128]{1,0:T(8,128)S(1)}, u32[]{:S(2)}, u32[]{:S(2)}) %collective-permute-start.10) | collective-permute-done | bytes 4128 | tf_op jit(solution)/shard_map/ppermute | solution.py:265
  38.0 0.0 collective-permute-done.9.even_ref
  38.0 0.8 %relax.1 = (f32[1,2,4,8]{3,2,1,0:T(4,128)}, f32[1,2,4,8]{3,2,1,0:T(4,128)}) custom-call(f32[8,128]{1,0:T(8,128)S(1)} %window.1.own_ref, f32[8,128]{1,0:T(8,128)S(1)} %collective-permute-done.9.even_ref, f32[8,128]{1,0:T(8,128)S(1)} %collective-permute-done.10.odd_ref), custom_call_target="tpu_custom_call" | custom-call | tf_op jit(solution)/shard_map/relax/pallas_call | solution.py:153
Async XLA Ops:
  0.6 1.0 %copy-start = (f32[1,256,512]{2,1,0:T(8,128)S(1)}, f32[1,256,512]{2,1,0:T(8,128)}, u32[]{:S(2)}) copy-start(f32[1,256,512]{2,1,0:T(8,128)} %param.4) | copy-start | bytes 1572868
  1.8 4.6 %collective-permute-start = (f32[32,512]{1,0:T(8,128)S(1)}, f32[32,512]{1,0:T(8,128)S(1)}, u32[]{:S(2)}, u32[]{:S(2)}) collective-permute-start(f32[32,512]{1,0:T(8,128)S(1)} %get-tuple-element.9), channel_id=1, source_target_pairs={{0,4},{4,0},{8,12},{12,8},{1,5},{5,1},{9,13},{13,9},{2,6},{6,2},{1... | collective-permute-start | bytes 196616 | tf_op jit(solution)/shard_map/ppermute | solution.py:260
  2.4 5.0 %collective-permute-start.1 = (f32[32,512]{1,0:T(8,128)S(1)}, f32[32,512]{1,0:T(8,128)S(1)}, u32[]{:S(2)}, u32[]{:S(2)}) collective-permute-start(f32[32,512]{1,0:T(8,128)S(1)} %get-tuple-element.10), channel_id=1, source_target_pairs={{0,12},{4,8},{8,4},{12,0},{1,13},{5,9},{9,5},{13,1},{2,14},{6,10},... | collective-permute-start | bytes 196616 | tf_op jit(solution)/shard_map/ppermute | solution.py:265
  5.0 14.4 %copy-start.1 = (bf16[2,256,256]{2,1,0:T(8,128)(2,1)S(1)}, bf16[2,256,256]{2,1,0:T(8,128)(2,1)}, u32[]{:S(2)}) copy-start(bf16[2,256,256]{2,1,0:T(8,128)(2,1)} %constant.7.clone.right) | copy-start | bytes 786436
  5.0 14.4 %copy-start.2 = (bf16[128,432]{1,0:T(8,128)(2,1)S(1)}, bf16[128,432]{1,0:T(8,128)(2,1)}, u32[]{:S(2)}) copy-start(bf16[128,432]{1,0:T(8,128)(2,1)} %constant.8.clone.back) | copy-start | bytes 331780
  5.0 14.4 %copy-start.3 = (bf16[144,384]{1,0:T(8,128)(2,1)S(1)}, bf16[144,384]{1,0:T(8,128)(2,1)}, u32[]{:S(2)}) copy-start(bf16[144,384]{1,0:T(8,128)(2,1)} %constant.6.clone.left) | copy-start | bytes 331780
  5.0 14.4 %collective-permute-start.4 = (f32[160,288]{1,0:T(8,128)S(1)}, f32[160,288]{1,0:T(8,128)S(1)}, u32[]{:S(2)}, u32[]{:S(2)}) collective-permute-start(f32[160,288]{1,0:T(8,128)S(1)} %get-tuple-element.13), channel_id=1, source_target_pairs={{0,16},{16,0},{17,1},{1,17},{2,18},{18,2},{19,3},{3,19},{4,20},{20... | collective-permute-start | bytes 552968 | tf_op jit(solution)/shard_map/ppermute | solution.py:243
  7.6 14.9 %collective-permute-start.5 = (f32[128,288]{1,0:T(8,128)S(1)}, f32[128,288]{1,0:T(8,128)S(1)}, u32[]{:S(2)}, u32[]{:S(2)}) collective-permute-start(f32[128,288]{1,0:T(8,128)S(1)} %get-tuple-element.14), channel_id=1, source_target_pairs={{0,16},{16,0},{17,1},{1,17},{2,18},{18,2},{19,3},{3,19},{4,20},{20... | collective-permute-start | bytes 442376 | tf_op jit(solution)/shard_map/ppermute | solution.py:243
  8.9 9.8 %collective-permute-start.2 = (f32[80,128]{1,0:T(8,128)S(1)}, f32[80,128]{1,0:T(8,128)S(1)}, u32[]{:S(2)}, u32[]{:S(2)}) collective-permute-start(f32[80,128]{1,0:T(8,128)S(1)} %get-tuple-element.11), channel_id=1, source_target_pairs={{0,3},{16,17},{17,16},{1,2},{2,1},{18,19},{19,18},{3,0},{4,7},{20,... | collective-permute-start | bytes 122888 | tf_op jit(solution)/shard_map/ppermute | solution.py:243
  12.7 6.7 %collective-permute-start.6 = (f32[80,128]{1,0:T(8,128)S(1)}, f32[80,128]{1,0:T(8,128)S(1)}, u32[]{:S(2)}, u32[]{:S(2)}) collective-permute-start(f32[80,128]{1,0:T(8,128)S(1)} %get-tuple-element.15), channel_id=1, source_target_pairs={{0,17},{16,3},{17,2},{1,16},{2,19},{18,1},{19,0},{3,18},{4,21},{20... | collective-permute-start | bytes 122888 | tf_op jit(solution)/shard_map/ppermute | solution.py:243
  12.7 6.0 %collective-permute-start.3 = (f32[32,288]{1,0:T(8,128)S(1)}, f32[32,288]{1,0:T(8,128)S(1)}, u32[]{:S(2)}, u32[]{:S(2)}) collective-permute-start(f32[32,288]{1,0:T(8,128)S(1)} %get-tuple-element.12), channel_id=1, source_target_pairs={{0,16},{16,0},{17,1},{1,17},{2,18},{18,2},{19,3},{3,19},{4,20},{20... | collective-permute-start | bytes 110600 | tf_op jit(solution)/shard_map/ppermute | solution.py:243
  25.8 5.4 %collective-permute-start.7 = (f32[8,128]{1,0:T(8,128)S(1)}, f32[8,128]{1,0:T(8,128)S(1)}, u32[]{:S(2)}, u32[]{:S(2)}) collective-permute-start(f32[8,128]{1,0:T(8,128)S(1)} %lower.1.own_ref), channel_id=1, source_target_pairs={{0,3},{16,17},{17,16},{1,2},{2,1},{18,19},{19,18},{3,0},{4,7},{20,... | collective-permute-start | bytes 12296 | tf_op jit(solution)/shard_map/ppermute | solution.py:243
  31.3 3.6 %collective-permute-start.8 = (f32[8,128]{1,0:T(8,128)S(1)}, f32[8,128]{1,0:T(8,128)S(1)}, u32[]{:S(2)}, u32[]{:S(2)}) collective-permute-start(f32[8,128]{1,0:T(8,128)S(1)} %close.1.own_ref), channel_id=1, source_target_pairs={{0,16},{16,0},{17,1},{1,17},{2,18},{18,2},{19,3},{3,19},{4,20},{20... | collective-permute-start | bytes 12296 | tf_op jit(solution)/shard_map/ppermute | solution.py:243
  35.0 3.0 %collective-permute-start.10 = (f32[8,128]{1,0:T(8,128)S(1)}, f32[8,128]{1,0:T(8,128)S(1)}, u32[]{:S(2)}, u32[]{:S(2)}) collective-permute-start(f32[8,128]{1,0:T(8,128)S(1)} %window.1.own_ref), channel_id=1, source_target_pairs={{0,12},{4,8},{8,4},{12,0},{1,13},{5,9},{9,5},{13,1},{2,14},{6,10},... | collective-permute-start | bytes 12296 | tf_op jit(solution)/shard_map/ppermute | solution.py:265
  35.0 3.0 %collective-permute-start.9 = (f32[8,128]{1,0:T(8,128)S(1)}, f32[8,128]{1,0:T(8,128)S(1)}, u32[]{:S(2)}, u32[]{:S(2)}) collective-permute-start(f32[8,128]{1,0:T(8,128)S(1)} %window.1.own_ref), channel_id=1, source_target_pairs={{0,4},{4,0},{8,12},{12,8},{1,5},{5,1},{9,13},{13,9},{2,6},{6,2},{1... | collective-permute-start | bytes 12296 | tf_op jit(solution)/shard_map/ppermute | solution.py:260
